TPU v7x, 32 devices: a whole 2x2x4 slice. The times are simulated.
32 devices in a mesh: ep: 8 (over y, x, core), dp: 4 (over z).
Axes of the slice: x: 2, y: 2, z: 4, core: 2. Of those that a mesh axis runs over, the one named last changes fastest.
Arguments:
- hidden: bfloat16 [8, 1024, 768], P('ep', 'dp'), may hold values from -6 to 6
- cotangent: bfloat16 [8, 1024, 2048], P('ep', 'dp'), may hold values from -0.796875 to 0.796875
- down_weight: bfloat16 [8, 768, 2048], P('ep', 'dp'), may hold values from -0.21875 to 0.21875
- slot_expert: int32 [8], replicated, may hold values from 0 to 127, as said below
- row_counts: int32 [8, 4], P('ep', 'dp'), may hold values from 128 to 256, as said below
Outputs:
- output: bfloat16 [8, 1024, 2048], P('ep', 'dp')
- hidden_grad: bfloat16 [8, 1024, 768], P('ep', 'dp')
- weight_grad: bfloat16 [8, 768, 2048], P('ep', 'dp')
Inputs may be any that keep to these rules, and one draw needn't show every extreme that they name: `slot_expert`: equal values form runs of 2 to 4 neighbouring slots, and runs of 2 occur; different runs carry different values. `row_counts`: multiples of 128; some entry equals 256 and some equals 128.
All inputs are finite; a program needn't handle non-finite values.
Results may differ from a plain program's by a relative error of at most 0.012.
Values may be sent and summed in bfloat16 or wider, within the bound.
No kernel may reach another device: no remote copies, remote signals or barrier semaphores. Data moves between devices by JAX's collectives and lax.ppermute only.
A program may use at most 64 MiB of HBM per device.

v0:
```python
import jax
import jax.numpy as jnp
from jax import lax
from jax.sharding import PartitionSpec as P


def shifted(x, axis, by):
    size = lax.axis_size(axis)
    pairs = [(i, i + by) for i in range(size) if 0 <= i + by < size]
    return lax.ppermute(x, axis, pairs)


def slot_layout(slot_expert, device_index):
    total_slots = slot_expert.shape[0]
    places = lax.iota(jnp.int32, total_slots)
    earlier = jnp.concatenate([slot_expert[:1] - 1, slot_expert[:-1]])
    begins = slot_expert != earlier
    group_ids = jnp.cumsum(begins.astype(jnp.int32)) - 1
    own_group = jnp.sum(jnp.where(places == device_index, group_ids, 0))
    same_group = group_ids == own_group
    first_slot = jnp.min(jnp.where(same_group, places, total_slots))
    members = jnp.sum(same_group.astype(jnp.int32))
    return (device_index - first_slot, members)


def shards(hidden, cotangent, down_weight, slot_expert, row_counts):
    device_index = lax.axis_index("ep")
    offset, members = slot_layout(slot_expert, device_index)
    capacity = hidden.shape[1]
    live_rows = (lax.iota(jnp.int32, capacity) < row_counts[0, 0])[:, None]
    masked_hidden = jnp.where(live_rows, hidden[0], jnp.zeros((), jnp.bfloat16))
    masked_grads = jnp.where(live_rows, cotangent[0], jnp.zeros((), jnp.bfloat16))
    weight_quarter = down_weight[0]
    current = weight_quarter
    for distance in (1, 2, 3):
        arrived = shifted(weight_quarter, "ep", distance)
        current = jnp.where(offset == distance, arrived, current)
    shard_rows = lax.all_gather(current, "dp", axis=0, tiled=True)
    columns = masked_hidden
    outputs = jnp.dot(columns, shard_rows, preferred_element_type=jnp.float32)
    columns_grad = lax.dot_general(
        masked_grads, shard_rows, (((1,), (1,)), ((), ())), preferred_element_type=jnp.float32
    )
    input_grads = columns_grad
    outputs, input_grads = (outputs, input_grads)
    columns = masked_hidden
    replica_sum = lax.psum_scatter(
        lax.dot_general(
            columns, masked_grads, (((0,), (0,)), ((), ())), preferred_element_type=jnp.float32
        ).astype(jnp.bfloat16),
        "dp",
        scatter_dimension=0,
        tiled=True,
    )
    summed = replica_sum.astype(jnp.float32)
    arrived_terms = shifted(replica_sum, "ep", -2)
    inside_far = (offset < 2) & (offset + 2 < members)
    summed = summed + jnp.where(inside_far, arrived_terms.astype(jnp.float32), 0.0)
    arrived_sums = shifted(summed.astype(jnp.bfloat16), "ep", -1).astype(summed.dtype)
    inside_near = (offset < 1) & (offset + 1 < members)
    summed = summed + jnp.where(inside_near, arrived_sums, 0.0)
    weight_grad = summed.astype(jnp.bfloat16)
    for distance in (1, 2):
        arrived = shifted(weight_grad, "ep", distance)
        weight_grad = jnp.where(offset >= distance, arrived, weight_grad)
    return (
        outputs.astype(jnp.bfloat16)[None],
        input_grads.astype(jnp.bfloat16)[None],
        weight_grad[None],
    )


def solution(mesh):
    return jax.shard_map(
        shards,
        mesh=mesh,
        in_specs=(
            P("ep", "dp", None),
            P("ep", "dp", None),
            P("ep", "dp", None),
            P(),
            P("ep", "dp"),
        ),
        out_specs=(P("ep", "dp", None), P("ep", "dp", None), P("ep", "dp", None)),
        check_vma=False,
    )
```

profile of v0, /device:TPU:0, one launch (start us, length us, event | category | flops | bytes accessed | tf_op | source)
XLA Modules:
  0.0 154.5 jit_solution(4497335765287746895)
XLA Ops:
  7.2 0.0 reduce-scatter.2.cloned.1.call-start
  7.9 4.1 %convolution_convert_fusion = bf16[768,2048]{1,0:T(8,128)(2,1)} fusion(bf16[1,256,2048]{2,1,0:T(8,128)(2,1)} %param.6, pred[256]{0:T(512)(128)(4,1)S(1)} %iota_compare_fusion, bf16[1,256,768]{2,1,0:T(8,128)(2,1)} %param.5), kind=kOutput, calls=%fused_computation | convolution fusion | flops 807600128 | bytes 4587776 | tf_op jit(solution)/shard_map/dot_general | solution.py:48
  12.0 0.0 copy-start.3
  12.0 0.0 copy-start.4
  12.0 0.0 reduce-scatter.2.cloned.1.call-update
  12.0 0.0 all-gather.2.cloned.1.call-start
  12.1 1.1 copy-done.3
  13.1 4.3 %collective-permute-start = (bf16[192,2048]{1,0:T(8,128)(2,1)S(1)}, bf16[192,2048]{1,0:T(8,128)(2,1)S(1)}, u32[]{:S(2)}, u32[]{:S(2)}) collective-permute-start(bf16[192,2048]{1,0:T(8,128)(2,1)S(1)} %bitcast.32), channel_id=1, source_target_pairs={{0,12},{4,16},{8,20},{12,24},{16,28},{1,13},{5,17},{9,21},{13,25},... | collective-permute-start | bytes 2359304 | tf_op jit(solution)/shard_map/ppermute | solution.py:10
  17.5 3.4 %collective-permute-start.1 = (bf16[192,2048]{1,0:T(8,128)(2,1)S(1)}, bf16[192,2048]{1,0:T(8,128)(2,1)S(1)}, u32[]{:S(2)}, u32[]{:S(2)}) collective-permute-start(bf16[192,2048]{1,0:T(8,128)(2,1)S(1)} %bitcast.33), channel_id=1, source_target_pairs={{0,8},{4,12},{8,16},{12,20},{16,24},{20,28},{1,9},{5,13},{9,17},{1... | collective-permute-start | bytes 2359304 | tf_op jit(solution)/shard_map/ppermute | solution.py:10
  21.0 2.3 %collective-permute-start.2 = (bf16[192,2048]{1,0:T(8,128)(2,1)S(1)}, bf16[192,2048]{1,0:T(8,128)(2,1)S(1)}, u32[]{:S(2)}, u32[]{:S(2)}) collective-permute-start(bf16[192,2048]{1,0:T(8,128)(2,1)S(1)} %bitcast.34), channel_id=1, source_target_pairs={{0,4},{4,8},{8,12},{12,16},{16,20},{20,24},{24,28},{1,5},{5,9},{9,... | collective-permute-start | bytes 2359304 | tf_op jit(solution)/shard_map/ppermute | solution.py:10
  23.3 0.0 copy-done.4
  23.3 0.1 fusion.17
  23.4 0.2 reduce-window.9
  23.6 0.6 fusion.18
  24.2 1.3 fusion.16
  26.2 6.0 %collective-permute-done = bf16[192,2048]{1,0:T(8,128)(2,1)S(1)} collective-permute-done((bf16[192,2048]{1,0:T(8,128)(2,1)S(1)}, bf16[192,2048]{1,0:T(8,128)(2,1)S(1)}, u32[]{:S(2)}, u32[]{:S(2)}) %collective-permute-start) | collective-permute-done | bytes 786464 | tf_op jit(solution)/shard_map/ppermute | solution.py:10
  32.2 16.9 %collective-permute-done.1 = bf16[192,2048]{1,0:T(8,128)(2,1)S(1)} collective-permute-done((bf16[192,2048]{1,0:T(8,128)(2,1)S(1)}, bf16[192,2048]{1,0:T(8,128)(2,1)S(1)}, u32[]{:S(2)}, u32[]{:S(2)}) %collective-permute-start.1) | collective-permute-done | bytes 786464 | tf_op jit(solution)/shard_map/ppermute | solution.py:10
  49.1 0.0 collective-permute-done.2
  49.1 1.0 select_select_fusion
  50.1 0.0 all-gather.2.cloned.1.call-update
  50.1 25.2 %reduce-scatter.2.cloned.1.call-done = bf16[192,2048]{1,0:T(8,128)(2,1)} async-done(((bf16[768,2048]{1,0:T(8,128)(2,1)}), bf16[192,2048]{1,0:T(8,128)(2,1)}) %reduce-scatter.2.cloned.1.call-update) | async-done | bytes 786448 | tf_op jit(solution)/shard_map/reduce_scatter | solution.py:47
  75.3 0.0 copy-start
  75.3 1.4 collective-permute-start.3
  77.4 19.0 %collective-permute-done.3 = bf16[192,2048]{1,0:T(8,128)(2,1)S(1)} collective-permute-done((bf16[192,2048]{1,0:T(8,128)(2,1)}, bf16[192,2048]{1,0:T(8,128)(2,1)S(1)}, u32[]{:S(2)}, u32[]{:S(2)}) %collective-permute-start.3) | collective-permute-done | bytes 786464 | tf_op jit(solution)/shard_map/ppermute | solution.py:10
  96.4 1.4 fusion.1
  97.9 1.3 collective-permute-start.4
  99.8 2.2 %collective-permute-done.4 = bf16[192,2048]{1,0:T(8,128)(2,1)S(1)} collective-permute-done((bf16[192,2048]{1,0:T(8,128)(2,1)S(1)}, bf16[192,2048]{1,0:T(8,128)(2,1)S(1)}, u32[]{:S(2)}, u32[]{:S(2)}) %collective-permute-start.4) | collective-permute-done | bytes 786464 | tf_op jit(solution)/shard_map/ppermute | solution.py:10
  102.1 0.0 copy-done
  102.1 0.5 add_convert_fusion
  102.5 0.0 copy-start.1
  102.5 12.4 %collective-permute-start.5 = (bf16[192,2048]{1,0:T(8,128)(2,1)S(1)}, bf16[192,2048]{1,0:T(8,128)(2,1)S(1)}, u32[]{:S(2)}, u32[]{:S(2)}) collective-permute-start(bf16[192,2048]{1,0:T(8,128)(2,1)S(1)} %add_convert_fusion), channel_id=1, source_target_pairs={{0,4},{4,8},{8,12},{12,16},{16,20},{20,24},{24,28},{1,5},{5,9},{9,... | collective-permute-start | bytes 2359304 | tf_op jit(solution)/shard_map/ppermute | solution.py:10
  114.9 1.8 %collective-permute-done.5 = bf16[192,2048]{1,0:T(8,128)(2,1)S(1)} collective-permute-done((bf16[192,2048]{1,0:T(8,128)(2,1)S(1)}, bf16[192,2048]{1,0:T(8,128)(2,1)S(1)}, u32[]{:S(2)}, u32[]{:S(2)}) %collective-permute-start.5) | collective-permute-done | bytes 786464 | tf_op jit(solution)/shard_map/ppermute | solution.py:10
  116.8 0.1 broadcast_select_fusion
  116.8 11.4 %collective-permute-start.6 = (bf16[192,2048]{1,0:T(8,128)(2,1)S(1)}, bf16[192,2048]{1,0:T(8,128)(2,1)S(1)}, u32[]{:S(2)}, u32[]{:S(2)}) collective-permute-start(bf16[192,2048]{1,0:T(8,128)(2,1)S(1)} %broadcast_select_fusion), channel_id=1, source_target_pairs={{0,8},{4,12},{8,16},{12,20},{16,24},{20,28},{1,9},{5,13},{9,17},{1... | collective-permute-start | bytes 2359304 | tf_op jit(solution)/shard_map/ppermute | solution.py:10
  128.2 0.0 copy-start.2
  128.2 12.7 %all-gather.2.cloned.1.call-done = bf16[768,2048]{1,0:T(8,128)(2,1)} async-done(((bf16[192,2048]{1,0:T(8,128)(2,1)}), bf16[768,2048]{1,0:T(8,128)(2,1)}) %all-gather.2.cloned.1.call-update) | async-done | bytes 3145744 | tf_op jit(solution)/shard_map/all_gather | solution.py:38
  140.9 0.0 copy-done.1
  140.9 0.0 copy-start.5
  140.9 4.0 %fusion = bf16[1,256,2048]{2,1,0:T(8,128)(2,1)} fusion(bf16[768,2048]{1,0:T(8,128)(2,1)} %all-gather.2.cloned.1.call-done, bf16[1,256,768]{2,1,0:T(8,128)(2,1)S(1)} %copy-done.1, pred[256]{0:T(512)(128)(4,1)S(1)} %iota_compare_fusion), kind=kOutput, calls=%fused_computation.2 | convolution fusion | flops 806027264 | bytes 4587776 | tf_op jit(solution)/shard_map/dot_general | solution.py:40
  144.9 0.0 copy-done.2
  144.9 0.0 copy-done.5
  144.9 1.8 %fusion.2 = bf16[1,256,768]{2,1,0:T(8,128)(2,1)} fusion(bf16[768,2048]{1,0:T(8,128)(2,1)S(1)} %copy-done.5, bf16[1,256,2048]{2,1,0:T(8,128)(2,1)S(1)} %copy-done.2, pred[256]{0:T(512)(128)(4,1)S(1)} %iota_compare_fusion), kind=kOutput, calls=%fused_computation.7 | convolution fusion | flops 806027264 | bytes 4587776 | tf_op jit(solution)/shard_map/dot_general | solution.py:41
  146.7 0.0 collective-permute-done.6
  146.7 1.0 select_bitcast_fusion
  (1 shorter events, 0.0 us)
Async XLA Ops:
  7.2 68.2 %reduce-scatter.2.cloned.1.call-start = ((), (), s32[]{:S(2)}) async-start(), calls=%async_computation.2 | async-start | bytes 3932160 | tf_op jit(solution)/shard_map/reduce_scatter | solution.py:47
  12.0 1.1 copy-start.3
  12.0 11.3 %copy-start.4 = (s32[8]{0:T(128)S(1)}, s32[8]{0:T(128)}, u32[]{:S(2)}) copy-start(s32[8]{0:T(128)} %param.8) | copy-start | bytes 100
  12.0 128.8 %all-gather.2.cloned.1.call-start = ((), (), s32[]{:S(2)}) async-start(), calls=%async_computation.1 | async-start | bytes 3932160 | tf_op jit(solution)/shard_map/all_gather | solution.py:38
  13.1 19.1 %collective-permute-start = (bf16[192,2048]{1,0:T(8,128)(2,1)S(1)}, bf16[192,2048]{1,0:T(8,128)(2,1)S(1)}, u32[]{:S(2)}, u32[]{:S(2)}) collective-permute-start(bf16[192,2048]{1,0:T(8,128)(2,1)S(1)} %bitcast.32), channel_id=1, source_target_pairs={{0,12},{4,16},{8,20},{12,24},{16,28},{1,13},{5,17},{9,21},{13,25},... | collective-permute-start | bytes 2359304 | tf_op jit(solution)/shard_map/ppermute | solution.py:10
  17.5 31.6 %collective-permute-start.1 = (bf16[192,2048]{1,0:T(8,128)(2,1)S(1)}, bf16[192,2048]{1,0:T(8,128)(2,1)S(1)}, u32[]{:S(2)}, u32[]{:S(2)}) collective-permute-start(bf16[192,2048]{1,0:T(8,128)(2,1)S(1)} %bitcast.33), channel_id=1, source_target_pairs={{0,8},{4,12},{8,16},{12,20},{16,24},{20,28},{1,9},{5,13},{9,17},{1... | collective-permute-start | bytes 2359304 | tf_op jit(solution)/shard_map/ppermute | solution.py:10
  21.0 28.1 %collective-permute-start.2 = (bf16[192,2048]{1,0:T(8,128)(2,1)S(1)}, bf16[192,2048]{1,0:T(8,128)(2,1)S(1)}, u32[]{:S(2)}, u32[]{:S(2)}) collective-permute-start(bf16[192,2048]{1,0:T(8,128)(2,1)S(1)} %bitcast.34), channel_id=1, source_target_pairs={{0,4},{4,8},{8,12},{12,16},{16,20},{20,24},{24,28},{1,5},{5,9},{9,... | collective-permute-start | bytes 2359304 | tf_op jit(solution)/shard_map/ppermute | solution.py:10
  75.3 26.7 %copy-start = (bf16[192,2048]{1,0:T(8,128)(2,1)S(1)}, bf16[192,2048]{1,0:T(8,128)(2,1)}, u32[]{:S(2)}) copy-start(bf16[192,2048]{1,0:T(8,128)(2,1)} %reduce-scatter.2.cloned.1.call-done) | copy-start | bytes 2359300
  75.3 21.1 %collective-permute-start.3 = (bf16[192,2048]{1,0:T(8,128)(2,1)}, bf16[192,2048]{1,0:T(8,128)(2,1)S(1)}, u32[]{:S(2)}, u32[]{:S(2)}) collective-permute-start(bf16[192,2048]{1,0:T(8,128)(2,1)} %reduce-scatter.2.cloned.1.call-done), channel_id=1, source_target_pairs={{8,0},{12,4},{16,8},{20,12},{24,16},{28,20},{9,1},{13,5},{17,9},{2... | collective-permute-start | bytes 2359304 | tf_op jit(solution)/shard_map/ppermute | solution.py:10
  97.9 4.2 %collective-permute-start.4 = (bf16[192,2048]{1,0:T(8,128)(2,1)S(1)}, bf16[192,2048]{1,0:T(8,128)(2,1)S(1)}, u32[]{:S(2)}, u32[]{:S(2)}) collective-permute-start(bf16[192,2048]{1,0:T(8,128)(2,1)S(1)} %fusion.1), channel_id=1, source_target_pairs={{4,0},{8,4},{12,8},{16,12},{20,16},{24,20},{28,24},{5,1},{9,5},{13... | collective-permute-start | bytes 2359304 | tf_op jit(solution)/shard_map/ppermute | solution.py:10
  102.5 38.3 %copy-start.1 = (bf16[1,256,768]{2,1,0:T(8,128)(2,1)S(1)}, bf16[1,256,768]{2,1,0:T(8,128)(2,1)}, u32[]{:S(2)}) copy-start(bf16[1,256,768]{2,1,0:T(8,128)(2,1)} %param.5) | copy-start | bytes 1179652
  102.5 14.2 %collective-permute-start.5 = (bf16[192,2048]{1,0:T(8,128)(2,1)S(1)}, bf16[192,2048]{1,0:T(8,128)(2,1)S(1)}, u32[]{:S(2)}, u32[]{:S(2)}) collective-permute-start(bf16[192,2048]{1,0:T(8,128)(2,1)S(1)} %add_convert_fusion), channel_id=1, source_target_pairs={{0,4},{4,8},{8,12},{12,16},{16,20},{20,24},{24,28},{1,5},{5,9},{9,... | collective-permute-start | bytes 2359304 | tf_op jit(solution)/shard_map/ppermute | solution.py:10
  116.8 29.9 %collective-permute-start.6 = (bf16[192,2048]{1,0:T(8,128)(2,1)S(1)}, bf16[192,2048]{1,0:T(8,128)(2,1)S(1)}, u32[]{:S(2)}, u32[]{:S(2)}) collective-permute-start(bf16[192,2048]{1,0:T(8,128)(2,1)S(1)} %broadcast_select_fusion), channel_id=1, source_target_pairs={{0,8},{4,12},{8,16},{12,20},{16,24},{20,28},{1,9},{5,13},{9,17},{1... | collective-permute-start | bytes 2359304 | tf_op jit(solution)/shard_map/ppermute | solution.py:10
  128.2 16.7 %copy-start.2 = (bf16[1,256,2048]{2,1,0:T(8,128)(2,1)S(1)}, bf16[1,256,2048]{2,1,0:T(8,128)(2,1)}, u32[]{:S(2)}) copy-start(bf16[1,256,2048]{2,1,0:T(8,128)(2,1)} %param.6) | copy-start | bytes 3145732
  140.9 4.0 %copy-start.5 = (bf16[768,2048]{1,0:T(8,128)(2,1)S(1)}, bf16[768,2048]{1,0:T(8,128)(2,1)}, u32[]{:S(2)}) copy-start(bf16[768,2048]{1,0:T(8,128)(2,1)} %all-gather.2.cloned.1.call-done) | copy-start | bytes 9437188
Sparse Core Ops, SparseCore 0:
  12.2 63.1 reduce-scatter.1
  77.5 63.3 all-gather.1
where the time goes:
time: 155 us
  waiting for transfers between devices  83.9 us (54%)
  starting transfers between devices  36.6 us (24%)
  between operations  16.8 us (11%)
  matrix products  9.96 us (6%)
  other arithmetic  6.14 us (4%)
    ppermute x7, waiting for transfers between devices, shifted(): return lax.ppermute(x, axis, pairs)  46 us
    ppermute x7, starting transfers between devices, shifted(): return lax.ppermute(x, axis, pairs)  36.5 us
    reduce_scatter x1, waiting for transfers between devices, shards(): lax.psum_scatter(lax.dot_general(columns, masked_grads, (((0,), (0,)), ((...  25.2 us
    all_gather x1, waiting for transfers between devices, shards(): shard_rows = lax.all_gather(current, 'dp', axis=0, tiled=True)  12.7 us
    dot_general x1, matrix products, shards(): lax.dot_general(columns, masked_grads, (((0,), (0,)), ((), ())), preferre...  4.14 us
    dot_general x1, matrix products, shards(): outputs = jnp.dot(columns, shard_rows, preferred_element_type=jnp.float32)  4.04 us
  transfers between devices with their start and end apart: 9, of which 7 were waited for; matrix products, arithmetic and copies ran while one was open for 7% of the time, Pallas kernels for 0%

commit v1 on v0

v1 whole, which is shorter than its diff:
```python
import jax
import jax.numpy as jnp
from jax import lax
from jax.sharding import PartitionSpec as P

BF16 = jnp.bfloat16
F32 = jnp.float32


def make_body(n_ep, n_dp):
    assert n_dp == 4 and n_ep % 2 == 0
    both = ("ep", "dp")
    core_pairs = [(s, s ^ 1) for s in range(n_ep)]
    help_pairs = [(s, s + 1 if s % 2 else s - 1) for s in range(2, n_ep - 2)]
    back_pairs = [(b, a) for a, b in help_pairs]
    right_two = [(s, s + 2) for s in range(n_ep - 2)]
    left_two = [(s + 2, s) for s in range(n_ep - 2)]
    right_four_weight = [(s - 4, s) for s in range(6, n_ep - 2, 2)]
    right_four_grad = [(s - 4, s) for s in range(7, n_ep - 2, 2)]
    left_four_grad = [(s + 4, s) for s in range(2, n_ep - 7, 2)]
    side_pairs = [(0, 1), (1, 0), (2, 3), (3, 2)]
    middle_pairs = []
    for s in range(n_ep):
        for z in range(n_dp):
            t, w = (s, z ^ 3) if z in (1, 2) else (s ^ 1, z)
            middle_pairs.append((s * n_dp + z, t * n_dp + w))

    def core(x):
        return lax.ppermute(x, "ep", core_pairs)

    def shift(x, pairs):
        return lax.ppermute(x, "ep", pairs) if pairs else jnp.zeros_like(x)

    def side(x):
        return lax.ppermute(x, "dp", side_pairs)

    def middle(x):
        return lax.ppermute(x, both, middle_pairs)

    def plus(a, b):
        return (a.astype(F32) + b.astype(F32)).astype(BF16)

    def body(hidden, cotangent, down_weight, slot_expert, row_counts):
        s = lax.axis_index("ep")
        z = lax.axis_index("dp")
        odd = (s % 2) == 1
        is_middle = (z == 1) | (z == 2)
        capacity, units = hidden.shape[1:]
        quarter, features = down_weight.shape[1:]
        half = features // 2
        pad = jnp.full((4,), -1, jnp.int32)
        window = lax.dynamic_slice(jnp.concatenate([pad, slot_expert, pad]), (s,), (9,))
        e = [window[k] for k in range(9)]
        own = e[4]
        eq = {d: e[4 + d] == own for d in (-3, -2, -1, 1, 2, 3)}
        with_partner = jnp.where(odd, eq[-1], eq[1])
        helps = jnp.where(odd, eq[1] & (e[6] != own), eq[-1] & (e[2] != own))

        def low(x):
            return jnp.where(odd, x[:, half:], x[:, :half])

        def high(x):
            return jnp.where(odd, x[:, :half], x[:, half:])

        stored = down_weight[0]
        own_part = low(stored)
        partner_part = core(high(stored))
        export = jnp.where(with_partner != odd, own_part, partner_part)
        came = shift(export, right_two)
        if right_four_weight:
            came = jnp.where(eq[-3] & ~odd, shift(export, right_four_weight), came)
        unit = jnp.where(
            ~eq[-1], own_part, jnp.where(odd & ~eq[-2], partner_part, came)
        )

        live = (lax.iota(jnp.int32, capacity) < row_counts[0, 0])[:, None]
        zero = jnp.zeros((), BF16)
        h = jnp.where(live, hidden[0], zero)
        c = jnp.where(live, cotangent[0], zero)
        sent = jnp.concatenate([h, high(c)], axis=1)
        from_core = core(sent)
        from_next = shift(sent, help_pairs)
        from_core = jnp.where(with_partner, from_core, zero)
        from_next = jnp.where(helps, from_next, zero)
        hs = jnp.concatenate([h, from_core[:, :units], from_next[:, :units]], axis=0)
        cs = jnp.concatenate([low(c), from_core[:, units:], from_next[:, units:]], axis=0)
        grads = lax.dot_general(
            hs, cs, (((0,), (0,)), ((), ())), preferred_element_type=F32
        ).astype(BF16)

        def term(k):
            return lax.dynamic_slice(grads, ((z ^ k) * quarter, 0), (quarter, half))

        a1 = side(unit)
        m1 = middle(unit)
        a2 = side(jnp.where(is_middle, m1, term(3)))
        m2 = middle(a1)
        a3 = side(jnp.where(is_middle, m2, term(2)))
        m3 = middle(plus(a2, term(2)))
        a4 = side(jnp.where(is_middle, plus(m3, term(1)), term(1)))
        m4 = middle(plus(a3, term(3)))

        by_xor = [unit, a1, jnp.where(is_middle, m2, a2), jnp.where(is_middle, m1, a3)]
        flip1, flip2 = (z % 2) == 1, z >= 2
        x = [jnp.where(flip1, by_xor[k ^ 1], by_xor[k]) for k in range(4)]
        x = [jnp.where(flip2, x[k ^ 2], x[k]) for k in range(4)]
        weight = jnp.concatenate(x, axis=0)
        outs = jnp.dot(hs, weight, preferred_element_type=F32).astype(BF16)
        hgs = lax.dot_general(
            cs, weight, (((1,), (1,)), ((), ())), preferred_element_type=F32
        )
        hgb = hgs[capacity:].astype(BF16)
        made = jnp.concatenate([outs[capacity:], hgb], axis=1)
        back = jnp.where(
            with_partner, core(made[:capacity]), shift(made[capacity:], back_pairs)
        )
        o, q = outs[:capacity], back[:, :half]
        output = jnp.concatenate([jnp.where(odd, q, o), jnp.where(odd, o, q)], axis=1)
        hidden_grad = (hgs[:capacity] + back[:, half:].astype(F32)).astype(BF16)

        total = a4.astype(F32) + term(0).astype(F32)
        total = total + jnp.where(is_middle, m4.astype(F32), 0.0)
        held = total.astype(BF16)
        left = shift(held, right_two).astype(F32)
        right = shift(held, left_two).astype(F32)
        group = total + jnp.where(eq[-2], left, 0.0) + jnp.where(eq[2], right, 0.0)
        other = jnp.where(odd, left, right)
        if right_four_grad:
            far = jnp.where(odd, shift(held, right_four_grad), shift(held, left_four_grad))
            far_in = jnp.where(odd, e[0] == e[3], e[8] == e[5])
            other = other + jnp.where(far_in, far.astype(F32), 0.0)
        group = group.astype(BF16)
        g = core(jnp.where(with_partner, group, other.astype(BF16)))
        weight_grad = jnp.concatenate(
            [jnp.where(odd, g, group), jnp.where(odd, group, g)], axis=1
        )
        return output[None], hidden_grad[None], weight_grad[None]

    return body


def solution(mesh):
    spec = P("ep", "dp", None)
    return jax.shard_map(
        make_body(mesh.shape["ep"], mesh.shape["dp"]),
        mesh=mesh,
        in_specs=(spec, spec, spec, P(), P("ep", "dp")),
        out_specs=(spec, spec, spec),
        check_vma=False,
    )
```

time: 155 us -> 129 us (0.83); the launches traced: 155 us -> 127 us
  waiting for transfers between devices: 83.9 us -> 29.4 us
  starting transfers between devices: 36.6 us -> 64.8 us
  other arithmetic: 6.14 us -> 16.2 us
  between operations: 16.8 us -> 9.11 us
  matrix products: 9.96 us -> 4.24 us
  local copies, waits for them, and re-layouts: 1.08 us -> 3.25 us
    ppermute x7 -> x17, starting transfers between devices: 36.5 us -> 64.8 us  [the longest x4 28.9 us: middle(): return lax.ppermute(x, both, middle_pairs)]
    reduce_scatter x1 -> x0, waiting for transfers between devices: 25.2 us -> none  [shards(): lax.psum_scatter(lax.dot_general(columns, masked_grads, (((0,), (0,)), ((...]
    ppermute x7 -> x17, waiting for transfers between devices: 46 us -> 29.4 us  [the longest x5 21.6 us: shift(): return lax.ppermute(x, 'ep', pairs) if pairs else jnp.zeros_like(x)]
    all_gather x1 -> x0, waiting for transfers between devices: 12.7 us -> none  [shards(): shard_rows = lax.all_gather(current, 'dp', axis=0, tiled=True)]
    select_n x2 -> x16, other arithmetic: 1.1 us -> 8.92 us  [the longest x1 2.19 us: body(): a4 = side(jnp.where(is_middle, plus(m3, term(1)), term(1)))]
    dot_general x3, matrix products: 9.96 us -> 4.24 us  [the longest x1 1.43 us: body(): lax.dot_general(cs, weight, (((1,), (1,)), ((), ())), preferred_element_t...]
    reduce_sum x2 -> x0, other arithmetic: 1.91 us -> none  [the longest x1 1.28 us: slot_layout(): members = jnp.sum(same_group.astype(jnp.int32))]
    broadcast_in_dim x1 -> x3, other arithmetic: 0.96 us -> 2.83 us  [body(): return (output[None], hidden_grad[None], weight_grad[None])]
  transfers between devices with their start and end apart: 9 -> 17, of which waited for: 7 -> 5; matrix products, arithmetic and copies ran while one was open for 7% -> 13% of each run, Pallas kernels for 0% -> 0%
where the time goes in v1:
time: 129 us; the launch traced here: 127 us
  starting transfers between devices  64.8 us (50%)
  waiting for transfers between devices  29.4 us (23%)
  other arithmetic  16.2 us (13%)
  between operations  9.11 us (7%)
  matrix products  4.24 us (3%)
  local copies, waits for them, and re-layouts  3.25 us (3%)
    ppermute x4, starting transfers between devices, middle(): return lax.ppermute(x, both, middle_pairs)  28.9 us
    ppermute x5, waiting for transfers between devices, shift(): return lax.ppermute(x, 'ep', pairs) if pairs else jnp.zeros_like(x)  21.6 us
    ppermute x4, starting transfers between devices, core(): return lax.ppermute(x, 'ep', core_pairs)  15.4 us
    ppermute x5, starting transfers between devices, shift(): return lax.ppermute(x, 'ep', pairs) if pairs else jnp.zeros_like(x)  10.8 us
    ppermute x4, starting transfers between devices, side(): return lax.ppermute(x, 'dp', side_pairs)  9.72 us
    ppermute x4, waiting for transfers between devices, side(): return lax.ppermute(x, 'dp', side_pairs)  6.07 us
    convert_element_type x2, other arithmetic, plus(): return (a.astype(F32) + b.astype(F32)).astype(BF16)  3.03 us
    broadcast_in_dim x3, other arithmetic, body(): return (output[None], hidden_grad[None], weight_grad[None])  2.83 us
  transfers between devices with their start and end apart: 17, of which 5 were waited for; matrix products, arithmetic and copies ran while one was open for 13% of the time, Pallas kernels for 0%

profile of v1, /device:TPU:0, one launch (start us, length us, event | category | flops | bytes accessed | tf_op | source)
XLA Modules:
  0.0 126.9 jit_solution(8945883111348238381)
XLA Ops:
  0.7 1.2 broadcast_select_fusion.10
  1.9 0.6 collective-permute-start.2
  3.1 0.0 copy-start.12
  3.1 0.1 bitcast_select_fusion
  3.3 0.9 broadcast_select_fusion.5
  4.2 0.1 bitcast_select_fusion.1
  4.3 1.0 pad_maximum_fusion.4
  5.3 0.0 collective-permute-start
  5.3 0.1 pad_add_fusion
  5.4 0.1 dynamic_slice.18
  5.4 0.6 fusion.15
  8.6 0.1 broadcast_select_fusion.7
  8.7 4.9 %collective-permute-start.3 = (bf16[192,1024]{1,0:T(8,128)(2,1)S(1)}, bf16[192,1024]{1,0:T(8,128)(2,1)S(1)}, u32[]{:S(2)}, u32[]{:S(2)}) collective-permute-start(bf16[192,1024]{1,0:T(8,128)(2,1)S(1)} %broadcast_select_fusion.7), channel_id=1, source_target_pairs={{0,8},{4,12},{8,16},{12,20},{16,24},{20,28},{1,9},{5,13},{9,17},{1... | collective-permute-start | bytes 1179656 | tf_op jit(solution)/shard_map/ppermute | solution.py:32
  13.6 1.6 %collective-permute-start.1 = (bf16[256,1792]{1,0:T(8,128)(2,1)}, bf16[256,1792]{1,0:T(8,128)(2,1)}, u32[]{:S(2)}, u32[]{:S(2)}) collective-permute-start(bf16[256,1792]{1,0:T(8,128)(2,1)} %pad_maximum_fusion.4), channel_id=1, source_target_pairs={{8,4},{12,16},{16,12},{20,24},{9,5},{13,17},{17,13},{21,25},{10,6}... | collective-permute-start | bytes 2752520 | tf_op jit(solution)/shard_map/ppermute | solution.py:32
  18.9 3.2 %collective-permute-done.3 = bf16[192,1024]{1,0:T(8,128)(2,1)S(1)} collective-permute-done((bf16[192,1024]{1,0:T(8,128)(2,1)S(1)}, bf16[192,1024]{1,0:T(8,128)(2,1)S(1)}, u32[]{:S(2)}, u32[]{:S(2)}) %collective-permute-start.3) | collective-permute-done | bytes 393248 | tf_op jit(solution)/shard_map/ppermute | solution.py:32
  22.1 0.1 select_select_fusion
  22.1 0.1 collective-permute-start.4
  22.2 3.1 %collective-permute-start.5 = (bf16[192,1024]{1,0:T(8,128)(2,1)S(1)}, bf16[192,1024]{1,0:T(8,128)(2,1)S(1)}, u32[]{:S(2)}, u32[]{:S(2)}) collective-permute-start(bf16[192,1024]{1,0:T(8,128)(2,1)S(1)} %select_select_fusion), channel_id=1, source_target_pairs={{0,1},{1,0},{2,3},{3,2},{4,5},{5,4},{6,7},{7,6},{8,9},{9,8},{10,11... | collective-permute-start | bytes 1179656 | tf_op jit(solution)/shard_map/ppermute | solution.py:35
  25.4 1.2 broadcast_select_fusion.2
  26.6 0.1 broadcast_select_fusion
  26.7 0.0 copy-start.2
  26.7 0.1 slice.95
  26.8 0.1 slice.96
  26.9 0.0 copy-start.6
  27.0 1.0 copy-done.2
  27.9 1.4 %convolution_convert_fusion.1 = bf16[768,1024]{1,0:T(8,128)(2,1)S(1)} fusion(bf16[256,1024]{1,0:T(8,128)(2,1)S(1)} %slice.96, bf16[256,1024]{1,0:T(8,128)(2,1)S(1)} %slice.95, bf16[256,1024]{1,0:T(8,128)(2,1)S(1)} %copy-done.2, bf16[256,768]{1,0:T(8,128)(2,1)S(1)} %slice.92, bf16[256,768]{1,0:T(8,128)(2,1)S(1)} %slice.91, ...), kind=kOutput, calls=%fused_computation.3 | convolution fusion | flops 1217003520 | bytes 4325376 | tf_op jit(solution)/shard_map/dot_general | solution.py:87
  29.4 0.9 broadcast_select_fusion.13
  30.3 4.6 %collective-permute-start.8 = (bf16[192,1024]{1,0:T(8,128)(2,1)}, bf16[192,1024]{1,0:T(8,128)(2,1)}, u32[]{:S(2)}, u32[]{:S(2)}) collective-permute-start(bf16[192,1024]{1,0:T(8,128)(2,1)} %broadcast_select_fusion.13), channel_id=1, source_target_pairs={{0,1},{1,0},{2,3},{3,2},{4,5},{5,4},{6,7},{7,6},{8,9},{9,8},{10,11... | collective-permute-start | bytes 1179656 | tf_op jit(solution)/shard_map/ppermute | solution.py:35
  34.9 14.9 %collective-permute-start.6 = (bf16[192,1024]{1,0:T(8,128)(2,1)S(1)}, bf16[192,1024]{1,0:T(8,128)(2,1)S(1)}, u32[]{:S(2)}, u32[]{:S(2)}) collective-permute-start(bf16[192,1024]{1,0:T(8,128)(2,1)S(1)} %collective-permute-done.5), channel_id=1, source_target_pairs={{0,4},{1,2},{2,1},{3,7},{4,0},{5,6},{6,5},{7,3},{8,12},{9,10},{10,... | collective-permute-start | bytes 1179656 | tf_op jit(solution)/shard_map/ppermute | solution.py:38
  49.8 1.9 %add_convert_fusion.2 = bf16[192,1024]{1,0:T(8,128)(2,1)} fusion(bf16[192,1024]{1,0:T(8,128)(2,1)} %collective-permute-done.8, bf16[768,1024]{1,0:T(8,128)(2,1)S(1)} %convolution_convert_fusion.1, s32[]{:T(128)S(6)} %select_n.236), kind=kLoop, calls=%fused_computation.29 | loop fusion | flops 786432 | bytes 1179652 | tf_op jit(solution)/shard_map/convert_element_type | solution.py:41
  51.7 5.6 %collective-permute-start.11 = (bf16[192,1024]{1,0:T(8,128)(2,1)}, bf16[192,1024]{1,0:T(8,128)(2,1)}, u32[]{:S(2)}, u32[]{:S(2)}) collective-permute-start(bf16[192,1024]{1,0:T(8,128)(2,1)} %add_convert_fusion.2), channel_id=1, source_target_pairs={{0,4},{1,2},{2,1},{3,7},{4,0},{5,6},{6,5},{7,3},{8,12},{9,10},{10,... | collective-permute-start | bytes 1179656 | tf_op jit(solution)/shard_map/ppermute | solution.py:38
  57.3 1.7 %collective-permute-done.11 = bf16[192,1024]{1,0:T(8,128)(2,1)} collective-permute-done((bf16[192,1024]{1,0:T(8,128)(2,1)}, bf16[192,1024]{1,0:T(8,128)(2,1)}, u32[]{:S(2)}, u32[]{:S(2)}) %collective-permute-start.11) | collective-permute-done | bytes 393248 | tf_op jit(solution)/shard_map/ppermute | solution.py:38
  59.0 2.2 %fusion.7 = (bf16[192,1024]{1,0:T(8,128)(2,1)}, bf16[192,1024]{1,0:T(8,128)(2,1)}) fusion(bf16[192,1024]{1,0:T(8,128)(2,1)} %collective-permute-done.11, bf16[768,1024]{1,0:T(8,128)(2,1)S(1)} %convolution_convert_fusion.1, s32[]{:T(128)S(6)} %select_n.254, pred[]{:T(512)S(6)} %or.3, bf16[192,1024]{1,0:T(8,128)(2,1)S(1)} %collective-permute-done.6, ...), kind=kLoop, calls=%fused_computation.31 | loop fusion | flops 1179648 | bytes 2359305 | tf_op jit(solution)/shard_map/jit(_where)/select_n | solution.py:100
  61.2 2.0 %collective-permute-start.12 = (bf16[192,1024]{1,0:T(8,128)(2,1)}, bf16[192,1024]{1,0:T(8,128)(2,1)S(1)}, u32[]{:S(2)}, u32[]{:S(2)}) collective-permute-start(bf16[192,1024]{1,0:T(8,128)(2,1)} %get-tuple-element.12), channel_id=1, source_target_pairs={{0,1},{1,0},{2,3},{3,2},{4,5},{5,4},{6,7},{7,6},{8,9},{9,8},{10,11... | collective-permute-start | bytes 1179656 | tf_op jit(solution)/shard_map/ppermute | solution.py:35
  63.2 6.1 %collective-permute-done.7 = bf16[192,1024]{1,0:T(8,128)(2,1)} collective-permute-done((bf16[192,1024]{1,0:T(8,128)(2,1)}, bf16[192,1024]{1,0:T(8,128)(2,1)}, u32[]{:S(2)}, u32[]{:S(2)}) %collective-permute-start.7) | collective-permute-done | bytes 393248 | tf_op jit(solution)/shard_map/ppermute | solution.py:35
  69.3 1.1 add_convert_fusion
  70.4 8.3 %collective-permute-start.13 = (bf16[192,1024]{1,0:T(8,128)(2,1)S(1)}, bf16[192,1024]{1,0:T(8,128)(2,1)S(1)}, u32[]{:S(2)}, u32[]{:S(2)}) collective-permute-start(bf16[192,1024]{1,0:T(8,128)(2,1)S(1)} %add_convert_fusion), channel_id=1, source_target_pairs={{0,4},{1,2},{2,1},{3,7},{4,0},{5,6},{6,5},{7,3},{8,12},{9,10},{10,... | collective-permute-start | bytes 1179656 | tf_op jit(solution)/shard_map/ppermute | solution.py:38
  78.7 1.2 broadcast_select_fusion.23
  80.0 0.0 copy-start.3
  80.0 0.0 copy-start.7
  80.0 0.1 broadcast_select_fusion.22
  80.1 0.9 copy-done.3
  81.0 0.2 copy-done.5
  81.2 0.2 copy-done.7
  81.4 1.4 %fusion.6 = f32[768,768]{1,0:T(8,128)S(1)} fusion(bf16[256,1024]{1,0:T(8,128)(2,1)S(1)} %copy-done.7, bf16[256,1024]{1,0:T(8,128)(2,1)S(1)} %copy-done.5, bf16[256,1024]{1,0:T(8,128)(2,1)S(1)} %copy-done.3, bf16[192,1024]{1,0:T(8,128)(2,1)S(1)} %get-tuple-element.16, bf16[192,1024]{1,0:T(8,128)(2,1)S(1)} %get-tuple-element.15, ...), kind=kOutput, calls=%fused_computation.30 | convolution fusion | flops 1218969600 | bytes 5505024 | tf_op jit(solution)/shard_map/dot_general | solution.py:109
  82.8 1.4 %convolution_convert_fusion = bf16[768,1024]{1,0:T(8,128)(2,1)S(1)} fusion(bf16[256,768]{1,0:T(8,128)(2,1)S(1)} %copy-done.11, bf16[256,768]{1,0:T(8,128)(2,1)S(1)} %copy-done.9, bf16[256,768]{1,0:T(8,128)(2,1)S(1)} %bitcast_select_fusion.1, bf16[192,1024]{1,0:T(8,128)(2,1)S(1)} %get-tuple-element.16, bf16[192,1024]{1,0:T(8,128)(2,1)S(1)} %get-tuple-element.15, ...), kind=kOutput, calls=%fused_computation.2 | convolution fusion | flops 1218576384 | bytes 4325376 | tf_op jit(solution)/shard_map/dot_general | solution.py:108
  84.2 0.1 slice.138
  84.3 0.1 slice.97
  84.4 0.1 pad_maximum_fusion.3
  84.5 0.7 collective-permute-start.10
  85.2 10.5 %collective-permute-start.9 = (bf16[256,1792]{1,0:T(8,128)(2,1)S(1)}, bf16[256,1792]{1,0:T(8,128)(2,1)S(1)}, u32[]{:S(2)}, u32[]{:S(2)}) collective-permute-start(bf16[256,1792]{1,0:T(8,128)(2,1)S(1)} %get-tuple-element.11), channel_id=1, source_target_pairs={{0,4},{4,0},{8,12},{12,8},{16,20},{20,16},{24,28},{28,24},{1,5},{5... | collective-permute-start | bytes 2752520 | tf_op jit(solution)/shard_map/ppermute | solution.py:29
  95.8 0.2 fusion.8
  96.0 2.3 %collective-permute-start.14 = (bf16[192,1024]{1,0:T(8,128)(2,1)S(1)}, bf16[192,1024]{1,0:T(8,128)(2,1)S(1)}, u32[]{:S(2)}, u32[]{:S(2)}) collective-permute-start(bf16[192,1024]{1,0:T(8,128)(2,1)S(1)} %fusion.8), channel_id=1, source_target_pairs={{0,8},{4,12},{8,16},{12,20},{16,24},{20,28},{1,9},{5,13},{9,17},{1... | collective-permute-start | bytes 1179656 | tf_op jit(solution)/shard_map/ppermute | solution.py:32
  98.2 1.3 %collective-permute-start.15 = (bf16[192,1024]{1,0:T(8,128)(2,1)S(1)}, bf16[192,1024]{1,0:T(8,128)(2,1)S(1)}, u32[]{:S(2)}, u32[]{:S(2)}) collective-permute-start(bf16[192,1024]{1,0:T(8,128)(2,1)S(1)} %fusion.8), channel_id=1, source_target_pairs={{8,0},{12,4},{16,8},{20,12},{24,16},{28,20},{9,1},{13,5},{17,9},{2... | collective-permute-start | bytes 1179656 | tf_op jit(solution)/shard_map/ppermute | solution.py:32
  100.7 7.0 %collective-permute-done.14 = bf16[192,1024]{1,0:T(8,128)(2,1)S(1)} collective-permute-done((bf16[192,1024]{1,0:T(8,128)(2,1)S(1)}, bf16[192,1024]{1,0:T(8,128)(2,1)S(1)}, u32[]{:S(2)}, u32[]{:S(2)}) %collective-permute-start.14) | collective-permute-done | bytes 393248 | tf_op jit(solution)/shard_map/ppermute | solution.py:32
  107.7 11.4 %collective-permute-done.15 = bf16[192,1024]{1,0:T(8,128)(2,1)S(1)} collective-permute-done((bf16[192,1024]{1,0:T(8,128)(2,1)S(1)}, bf16[192,1024]{1,0:T(8,128)(2,1)S(1)}, u32[]{:S(2)}, u32[]{:S(2)}) %collective-permute-start.15) | collective-permute-done | bytes 393248 | tf_op jit(solution)/shard_map/ppermute | solution.py:32
  119.1 0.4 fusion.10
  119.6 4.3 %collective-permute-start.16 = (bf16[192,1024]{1,0:T(8,128)(2,1)S(1)}, bf16[192,1024]{1,0:T(8,128)(2,1)S(1)}, u32[]{:S(2)}, u32[]{:S(2)}) collective-permute-start(bf16[192,1024]{1,0:T(8,128)(2,1)S(1)} %get-tuple-element.3), channel_id=1, source_target_pairs={{0,4},{4,0},{8,12},{12,8},{16,20},{20,16},{24,28},{28,24},{1,5},{5... | collective-permute-start | bytes 1179656 | tf_op jit(solution)/shard_map/ppermute | solution.py:29
  123.8 0.1 broadcast_select_fusion.1
  123.9 0.1 broadcast_select_fusion.4
  124.0 1.1 maximum_bitcast_fusion
  125.1 0.8 fusion.9
  125.9 0.1 broadcast_select_fusion.9
  126.0 0.9 maximum_bitcast_fusion.1
  (36 shorter events, 0.1 us)
Async XLA Ops:
  0.6 2.5 %copy-start.1 = (bf16[1,256,2048]{2,1,0:T(8,128)(2,1)S(1)}, bf16[1,256,2048]{2,1,0:T(8,128)(2,1)}, u32[]{:S(2)}) copy-start(bf16[1,256,2048]{2,1,0:T(8,128)(2,1)} %param.6) | copy-start | bytes 3145732
  1.9 6.7 %collective-permute-start.2 = (bf16[192,1024]{1,0:T(8,128)(2,1)S(1)}, bf16[192,1024]{1,0:T(8,128)(2,1)S(1)}, u32[]{:S(2)}, u32[]{:S(2)}) collective-permute-start(bf16[192,1024]{1,0:T(8,128)(2,1)S(1)} %broadcast_select_fusion.10), channel_id=1, source_target_pairs={{0,4},{4,0},{8,12},{12,8},{16,20},{20,16},{24,28},{28,24},{1,5},{5... | collective-permute-start | bytes 1179656 | tf_op jit(solution)/shard_map/ppermute | solution.py:29
  3.1 1.0 copy-start.12
  4.2 1.1 copy-start.13
  4.2 4.4 %copy-start = (bf16[1,192,2048]{2,1,0:T(8,128)(2,1)S(1)}, bf16[1,192,2048]{2,1,0:T(8,128)(2,1)}, u32[]{:S(2)}) copy-start(bf16[1,192,2048]{2,1,0:T(8,128)(2,1)} %param.7) | copy-start | bytes 2359300
  5.3 20.1 %collective-permute-start = (bf16[256,1792]{1,0:T(8,128)(2,1)}, bf16[256,1792]{1,0:T(8,128)(2,1)}, u32[]{:S(2)}, u32[]{:S(2)}) collective-permute-start(bf16[256,1792]{1,0:T(8,128)(2,1)} %pad_maximum_fusion.4), channel_id=1, source_target_pairs={{0,4},{4,0},{8,12},{12,8},{16,20},{20,16},{24,28},{28,24},{1,5},{5... | collective-permute-start | bytes 2752520 | tf_op jit(solution)/shard_map/ppermute | solution.py:29
  8.7 13.4 %collective-permute-start.3 = (bf16[192,1024]{1,0:T(8,128)(2,1)S(1)}, bf16[192,1024]{1,0:T(8,128)(2,1)S(1)}, u32[]{:S(2)}, u32[]{:S(2)}) collective-permute-start(bf16[192,1024]{1,0:T(8,128)(2,1)S(1)} %broadcast_select_fusion.7), channel_id=1, source_target_pairs={{0,8},{4,12},{8,16},{12,20},{16,24},{20,28},{1,9},{5,13},{9,17},{1... | collective-permute-start | bytes 1179656 | tf_op jit(solution)/shard_map/ppermute | solution.py:32
  13.6 13.1 %collective-permute-start.1 = (bf16[256,1792]{1,0:T(8,128)(2,1)}, bf16[256,1792]{1,0:T(8,128)(2,1)}, u32[]{:S(2)}, u32[]{:S(2)}) collective-permute-start(bf16[256,1792]{1,0:T(8,128)(2,1)} %pad_maximum_fusion.4), channel_id=1, source_target_pairs={{8,4},{12,16},{16,12},{20,24},{9,5},{13,17},{17,13},{21,25},{10,6}... | collective-permute-start | bytes 2752520 | tf_op jit(solution)/shard_map/ppermute | solution.py:32
  22.1 7.2 %collective-permute-start.4 = (bf16[192,1024]{1,0:T(8,128)(2,1)S(1)}, bf16[192,1024]{1,0:T(8,128)(2,1)S(1)}, u32[]{:S(2)}, u32[]{:S(2)}) collective-permute-start(bf16[192,1024]{1,0:T(8,128)(2,1)S(1)} %select_select_fusion), channel_id=1, source_target_pairs={{0,4},{1,2},{2,1},{3,7},{4,0},{5,6},{6,5},{7,3},{8,12},{9,10},{10,... | collective-permute-start | bytes 1179656 | tf_op jit(solution)/shard_map/ppermute | solution.py:38
  22.2 12.7 %collective-permute-start.5 = (bf16[192,1024]{1,0:T(8,128)(2,1)S(1)}, bf16[192,1024]{1,0:T(8,128)(2,1)S(1)}, u32[]{:S(2)}, u32[]{:S(2)}) collective-permute-start(bf16[192,1024]{1,0:T(8,128)(2,1)S(1)} %select_select_fusion), channel_id=1, source_target_pairs={{0,1},{1,0},{2,3},{3,2},{4,5},{5,4},{6,7},{7,6},{8,9},{9,8},{10,11... | collective-permute-start | bytes 1179656 | tf_op jit(solution)/shard_map/ppermute | solution.py:35
  26.7 1.2 copy-start.2
  26.8 2.6 %copy-start.4 = (bf16[256,1024]{1,0:T(8,128)(2,1)}, bf16[256,1024]{1,0:T(8,128)(2,1)S(1)}, u32[]{:S(2)}) copy-start(bf16[256,1024]{1,0:T(8,128)(2,1)S(1)} %slice.95) | copy-start | bytes 1572868
  26.8 2.5 %copy-start.8 = (bf16[256,768]{1,0:T(8,128)(2,1)}, bf16[256,768]{1,0:T(8,128)(2,1)S(1)}, u32[]{:S(2)}) copy-start(bf16[256,768]{1,0:T(8,128)(2,1)S(1)} %slice.91) | copy-start | bytes 1179652
  26.9 2.5 %copy-start.6 = (bf16[256,1024]{1,0:T(8,128)(2,1)}, bf16[256,1024]{1,0:T(8,128)(2,1)S(1)}, u32[]{:S(2)}) copy-start(bf16[256,1024]{1,0:T(8,128)(2,1)S(1)} %slice.96) | copy-start | bytes 1572868
  26.9 2.4 %copy-start.10 = (bf16[256,768]{1,0:T(8,128)(2,1)}, bf16[256,768]{1,0:T(8,128)(2,1)S(1)}, u32[]{:S(2)}) copy-start(bf16[256,768]{1,0:T(8,128)(2,1)S(1)} %slice.92) | copy-start | bytes 1179652
  30.3 19.4 %collective-permute-start.8 = (bf16[192,1024]{1,0:T(8,128)(2,1)}, bf16[192,1024]{1,0:T(8,128)(2,1)}, u32[]{:S(2)}, u32[]{:S(2)}) collective-permute-start(bf16[192,1024]{1,0:T(8,128)(2,1)} %broadcast_select_fusion.13), channel_id=1, source_target_pairs={{0,1},{1,0},{2,3},{3,2},{4,5},{5,4},{6,7},{7,6},{8,9},{9,8},{10,11... | collective-permute-start | bytes 1179656 | tf_op jit(solution)/shard_map/ppermute | solution.py:35
  34.9 22.4 %collective-permute-start.6 = (bf16[192,1024]{1,0:T(8,128)(2,1)S(1)}, bf16[192,1024]{1,0:T(8,128)(2,1)S(1)}, u32[]{:S(2)}, u32[]{:S(2)}) collective-permute-start(bf16[192,1024]{1,0:T(8,128)(2,1)S(1)} %collective-permute-done.5), channel_id=1, source_target_pairs={{0,4},{1,2},{2,1},{3,7},{4,0},{5,6},{6,5},{7,3},{8,12},{9,10},{10,... | collective-permute-start | bytes 1179656 | tf_op jit(solution)/shard_map/ppermute | solution.py:38
  51.7 7.3 %collective-permute-start.11 = (bf16[192,1024]{1,0:T(8,128)(2,1)}, bf16[192,1024]{1,0:T(8,128)(2,1)}, u32[]{:S(2)}, u32[]{:S(2)}) collective-permute-start(bf16[192,1024]{1,0:T(8,128)(2,1)} %add_convert_fusion.2), channel_id=1, source_target_pairs={{0,4},{1,2},{2,1},{3,7},{4,0},{5,6},{6,5},{7,3},{8,12},{9,10},{10,... | collective-permute-start | bytes 1179656 | tf_op jit(solution)/shard_map/ppermute | solution.py:38
  61.2 8.1 %collective-permute-start.7 = (bf16[192,1024]{1,0:T(8,128)(2,1)}, bf16[192,1024]{1,0:T(8,128)(2,1)}, u32[]{:S(2)}, u32[]{:S(2)}) collective-permute-start(bf16[192,1024]{1,0:T(8,128)(2,1)} %get-tuple-element.13), channel_id=1, source_target_pairs={{0,1},{1,0},{2,3},{3,2},{4,5},{5,4},{6,7},{7,6},{8,9},{9,8},{10,11... | collective-permute-start | bytes 1179656 | tf_op jit(solution)/shard_map/ppermute | solution.py:35
  61.2 34.5 %collective-permute-start.12 = (bf16[192,1024]{1,0:T(8,128)(2,1)}, bf16[192,1024]{1,0:T(8,128)(2,1)S(1)}, u32[]{:S(2)}, u32[]{:S(2)}) collective-permute-start(bf16[192,1024]{1,0:T(8,128)(2,1)} %get-tuple-element.12), channel_id=1, source_target_pairs={{0,1},{1,0},{2,3},{3,2},{4,5},{5,4},{6,7},{7,6},{8,9},{9,8},{10,11... | collective-permute-start | bytes 1179656 | tf_op jit(solution)/shard_map/ppermute | solution.py:35
  70.4 25.3 %collective-permute-start.13 = (bf16[192,1024]{1,0:T(8,128)(2,1)S(1)}, bf16[192,1024]{1,0:T(8,128)(2,1)S(1)}, u32[]{:S(2)}, u32[]{:S(2)}) collective-permute-start(bf16[192,1024]{1,0:T(8,128)(2,1)S(1)} %add_convert_fusion), channel_id=1, source_target_pairs={{0,4},{1,2},{2,1},{3,7},{4,0},{5,6},{6,5},{7,3},{8,12},{9,10},{10,... | collective-permute-start | bytes 1179656 | tf_op jit(solution)/shard_map/ppermute | solution.py:38
  80.0 1.0 copy-start.3
  80.0 1.2 copy-start.5
  80.0 1.3 %copy-start.7 = (bf16[256,1024]{1,0:T(8,128)(2,1)S(1)}, bf16[256,1024]{1,0:T(8,128)(2,1)}, u32[]{:S(2)}) copy-start(bf16[256,1024]{1,0:T(8,128)(2,1)} %copy-done.6) | copy-start | bytes 1572868
  81.3 1.4 %copy-start.9 = (bf16[256,768]{1,0:T(8,128)(2,1)S(1)}, bf16[256,768]{1,0:T(8,128)(2,1)}, u32[]{:S(2)}) copy-start(bf16[256,768]{1,0:T(8,128)(2,1)} %copy-done.8) | copy-start | bytes 1179652
  81.3 1.4 %copy-start.11 = (bf16[256,768]{1,0:T(8,128)(2,1)S(1)}, bf16[256,768]{1,0:T(8,128)(2,1)}, u32[]{:S(2)}) copy-start(bf16[256,768]{1,0:T(8,128)(2,1)} %copy-done.10) | copy-start | bytes 1179652
  84.5 39.3 %collective-permute-start.10 = (bf16[256,1792]{1,0:T(8,128)(2,1)S(1)}, bf16[256,1792]{1,0:T(8,128)(2,1)S(1)}, u32[]{:S(2)}, u32[]{:S(2)}) collective-permute-start(bf16[256,1792]{1,0:T(8,128)(2,1)S(1)} %get-tuple-element.10), channel_id=1, source_target_pairs={{4,8},{16,12},{12,16},{24,20},{5,9},{17,13},{13,17},{25,21},{6,10}... | collective-permute-start | bytes 2752520 | tf_op jit(solution)/shard_map/ppermute | solution.py:32
  85.2 38.6 %collective-permute-start.9 = (bf16[256,1792]{1,0:T(8,128)(2,1)S(1)}, bf16[256,1792]{1,0:T(8,128)(2,1)S(1)}, u32[]{:S(2)}, u32[]{:S(2)}) collective-permute-start(bf16[256,1792]{1,0:T(8,128)(2,1)S(1)} %get-tuple-element.11), channel_id=1, source_target_pairs={{0,4},{4,0},{8,12},{12,8},{16,20},{20,16},{24,28},{28,24},{1,5},{5... | collective-permute-start | bytes 2752520 | tf_op jit(solution)/shard_map/ppermute | solution.py:29
  96.0 11.7 %collective-permute-start.14 = (bf16[192,1024]{1,0:T(8,128)(2,1)S(1)}, bf16[192,1024]{1,0:T(8,128)(2,1)S(1)}, u32[]{:S(2)}, u32[]{:S(2)}) collective-permute-start(bf16[192,1024]{1,0:T(8,128)(2,1)S(1)} %fusion.8), channel_id=1, source_target_pairs={{0,8},{4,12},{8,16},{12,20},{16,24},{20,28},{1,9},{5,13},{9,17},{1... | collective-permute-start | bytes 1179656 | tf_op jit(solution)/shard_map/ppermute | solution.py:32
  98.2 20.9 %collective-permute-start.15 = (bf16[192,1024]{1,0:T(8,128)(2,1)S(1)}, bf16[192,1024]{1,0:T(8,128)(2,1)S(1)}, u32[]{:S(2)}, u32[]{:S(2)}) collective-permute-start(bf16[192,1024]{1,0:T(8,128)(2,1)S(1)} %fusion.8), channel_id=1, source_target_pairs={{8,0},{12,4},{16,8},{20,12},{24,16},{28,20},{9,1},{13,5},{17,9},{2... | collective-permute-start | bytes 1179656 | tf_op jit(solution)/shard_map/ppermute | solution.py:32
  119.6 6.4 %collective-permute-start.16 = (bf16[192,1024]{1,0:T(8,128)(2,1)S(1)}, bf16[192,1024]{1,0:T(8,128)(2,1)S(1)}, u32[]{:S(2)}, u32[]{:S(2)}) collective-permute-start(bf16[192,1024]{1,0:T(8,128)(2,1)S(1)} %get-tuple-element.3), channel_id=1, source_target_pairs={{0,4},{4,0},{8,12},{12,8},{16,20},{20,16},{24,28},{28,24},{1,5},{5... | collective-permute-start | bytes 1179656 | tf_op jit(solution)/shard_map/ppermute | solution.py:29

commit v2 on v1

--- a/solution.py
+++ b/solution.py
@@ -13,6 +13,12 @@
     core_pairs = [(s, s ^ 1) for s in range(n_ep)]
     help_pairs = [(s, s + 1 if s % 2 else s - 1) for s in range(2, n_ep - 2)]
     back_pairs = [(b, a) for a, b in help_pairs]
+    far = [(a, b) for a, b in help_pairs if {a % 8, b % 8} == {3, 4}]
+    relays = {a ^ 5 for a, b in far}
+    near = [(a, b) for a, b in help_pairs if (a, b) not in far]
+    hop_one = [(a, a ^ 5) for a, b in far] + [p for p in near if p[0] in relays]
+    hop_two = [(a ^ 5, b) for a, b in far] + [p for p in near if p[0] not in relays]
+    hop_one_ends = [b for a, b in near if a in relays]
     right_two = [(s, s + 2) for s in range(n_ep - 2)]
     left_two = [(s + 2, s) for s in range(n_ep - 2)]
     right_four_weight = [(s - 4, s) for s in range(6, n_ep - 2, 2)]
@@ -56,11 +62,13 @@
         with_partner = jnp.where(odd, eq[-1], eq[1])
         helps = jnp.where(odd, eq[1] & (e[6] != own), eq[-1] & (e[2] != own))
 
+        own_at = (s % 2) * half
+
         def low(x):
-            return jnp.where(odd, x[:, half:], x[:, :half])
+            return lax.dynamic_slice(x, (0, own_at), (x.shape[0], half))
 
         def high(x):
-            return jnp.where(odd, x[:, :half], x[:, half:])
+            return lax.dynamic_slice(x, (0, half - own_at), (x.shape[0], half))
 
         stored = down_weight[0]
         own_part = low(stored)
@@ -79,17 +87,34 @@
         c = jnp.where(live, cotangent[0], zero)
         sent = jnp.concatenate([h, high(c)], axis=1)
         from_core = core(sent)
-        from_next = shift(sent, help_pairs)
-        from_core = jnp.where(with_partner, from_core, zero)
-        from_next = jnp.where(helps, from_next, zero)
+        is_relay = jnp.isin(s, jnp.array(sorted(relays), jnp.int32)) if relays else False
+        first = shift(sent, hop_one)
+        from_next = shift(jnp.where(is_relay, first, sent), hop_two)
+        if hop_one_ends:
+            by_one = jnp.isin(s, jnp.array(hop_one_ends, jnp.int32))
+            from_next = jnp.where(by_one, first, from_next)
         hs = jnp.concatenate([h, from_core[:, :units], from_next[:, :units]], axis=0)
-        cs = jnp.concatenate([low(c), from_core[:, units:], from_next[:, units:]], axis=0)
+        cs = jnp.concatenate(
+            [
+                low(c),
+                jnp.where(with_partner, from_core[:, units:], zero),
+                jnp.where(helps, from_next[:, units:], zero),
+            ],
+            axis=0,
+        )
         grads = lax.dot_general(
             hs, cs, (((0,), (0,)), ((), ())), preferred_element_type=F32
         ).astype(BF16)
 
+        terms = lax.optimization_barrier(
+            [
+                lax.dynamic_slice(grads, ((z ^ k) * quarter, 0), (quarter, half))
+                for k in range(4)
+            ]
+        )
+
         def term(k):
-            return lax.dynamic_slice(grads, ((z ^ k) * quarter, 0), (quarter, half))
+            return terms[k]
 
         a1 = side(unit)
         m1 = middle(unit)

time: 129 us -> 115 us (0.89)
  the two profiles are of different devices: /device:TPU:0 before, /device:TPU:15 now
where the time goes in v2:
time: 115 us
  waiting for transfers between devices  42.6 us (37%)
  starting transfers between devices  35.3 us (31%)
  other arithmetic  16.9 us (15%)
  between operations  9.24 us (8%)
  local copies, waits for them, and re-layouts  6.45 us (6%)
  matrix products  4.25 us (4%)
    ppermute x6, waiting for transfers between devices, shift(): return lax.ppermute(x, 'ep', pairs) if pairs else jnp.zeros_like(x)  19.3 us
    ppermute x4, starting transfers between devices, core(): return lax.ppermute(x, 'ep', core_pairs)  14.6 us
    ppermute x4, waiting for transfers between devices, side(): return lax.ppermute(x, 'dp', side_pairs)  12.5 us
    ppermute x4, waiting for transfers between devices, middle(): return lax.ppermute(x, both, middle_pairs)  10.8 us
    ppermute x6, starting transfers between devices, shift(): return lax.ppermute(x, 'ep', pairs) if pairs else jnp.zeros_like(x)  10.6 us
    ppermute x4, starting transfers between devices, middle(): return lax.ppermute(x, both, middle_pairs)  7.06 us
    ppermute x4, starting transfers between devices, side(): return lax.ppermute(x, 'dp', side_pairs)  3.03 us
    broadcast_in_dim x3, other arithmetic, body(): return (output[None], hidden_grad[None], weight_grad[None])  2.83 us
  transfers between devices with their start and end apart: 18, of which 9 were waited for; matrix products, arithmetic and copies ran while one was open for 12% of the time, Pallas kernels for 0%

profile of v2, /device:TPU:15, one launch (start us, length us, event | category | flops | bytes accessed | tf_op | source)
XLA Modules:
  0.0 114.7 jit_solution(1287816969279479788)
XLA Ops:
  1.3 1.1 bitcast_select_fusion.3
  2.4 1.4 %bitcast_select_fusion = bf16[256,2048]{1,0:T(8,128)(2,1)S(1)} fusion(bf16[1,256,2048]{2,1,0:T(8,128)(2,1)} %param.7, pred[256]{0:T(512)(128)(4,1)S(1)} %iota_compare_fusion), kind=kLoop, calls=%fused_computation.9 | loop fusion | flops 524288 | bytes 2097408 | tf_op jit(solution)/shard_map/jit(_where)/select_n | solution.py:87
  3.8 0.9 constant_dynamic-slice_fusion.4
  4.7 1.0 pad_maximum_fusion.4
  5.7 0.7 collective-permute-start.1
  6.4 1.3 %collective-permute-start.3 = (bf16[192,1024]{1,0:T(8,128)(2,1)S(1)}, bf16[192,1024]{1,0:T(8,128)(2,1)S(1)}, u32[]{:S(2)}, u32[]{:S(2)}) collective-permute-start(bf16[192,1024]{1,0:T(8,128)(2,1)S(1)} %dynamic-slice_bitcast_fusion), channel_id=1, source_target_pairs={{0,4},{4,0},{8,12},{12,8},{16,20},{20,16},{24,28},{28,24},{1,5},{5... | collective-permute-start | bytes 1179656 | tf_op jit(solution)/shard_map/ppermute | solution.py:35
  7.8 0.1 collective-permute-start
  7.8 0.1 pad_add_fusion
  7.9 0.1 dynamic_slice.31
  8.0 0.7 fusion.15
  11.2 0.6 compare_reduce_fusion
  11.8 0.1 bitcast_select_fusion.2
  12.0 1.3 %collective-permute-start.4 = (bf16[192,1024]{1,0:T(8,128)(2,1)S(1)}, bf16[192,1024]{1,0:T(8,128)(2,1)}, u32[]{:S(2)}, u32[]{:S(2)}) collective-permute-start(bf16[192,1024]{1,0:T(8,128)(2,1)S(1)} %bitcast_select_fusion.2), channel_id=1, source_target_pairs={{0,8},{4,12},{8,16},{12,20},{16,24},{20,28},{1,9},{5,13},{9,17},{1... | collective-permute-start | bytes 1179656 | tf_op jit(solution)/shard_map/ppermute | solution.py:38
  13.3 1.8 %broadcast_select_fusion = bf16[256,1792]{1,0:T(8,128)(2,1)} fusion(bf16[256,1792]{1,0:T(8,128)(2,1)S(1)} %collective-permute-done.1, pred[]{:T(512)} %compare_reduce_fusion, bf16[256,1024]{1,0:T(8,128)(2,1)S(1)} %get-tuple-element.28, bf16[256,768]{1,0:T(8,128)(2,1)S(1)} %bitcast_select_fusion.3), kind=kLoop, calls=%fused_computation.16 | loop fusion | flops 2293760 | bytes 2752513 | tf_op jit(solution)/shard_map/jit(_where)/select_n | solution.py:92
  15.1 1.6 %collective-permute-start.2 = (bf16[256,1792]{1,0:T(8,128)(2,1)}, bf16[256,1792]{1,0:T(8,128)(2,1)}, u32[]{:S(2)}, u32[]{:S(2)}) collective-permute-start(bf16[256,1792]{1,0:T(8,128)(2,1)} %broadcast_select_fusion), channel_id=1, source_target_pairs={{24,16},{4,12},{8,4},{20,24},{25,17},{5,13},{9,5},{21,25},{26,18},... | collective-permute-start | bytes 2752520 | tf_op jit(solution)/shard_map/ppermute | solution.py:38
  18.0 6.2 %collective-permute-done.4 = bf16[192,1024]{1,0:T(8,128)(2,1)} collective-permute-done((bf16[192,1024]{1,0:T(8,128)(2,1)S(1)}, bf16[192,1024]{1,0:T(8,128)(2,1)}, u32[]{:S(2)}, u32[]{:S(2)}) %collective-permute-start.4) | collective-permute-done | bytes 393248 | tf_op jit(solution)/shard_map/ppermute | solution.py:38
  24.2 0.2 bitcast_select_fusion.1
  24.4 0.2 collective-permute-start.6
  27.2 2.5 %collective-permute-start.5 = (bf16[192,1024]{1,0:T(8,128)(2,1)S(1)}, bf16[192,1024]{1,0:T(8,128)(2,1)S(1)}, u32[]{:S(2)}, u32[]{:S(2)}) collective-permute-start(bf16[192,1024]{1,0:T(8,128)(2,1)S(1)} %bitcast_select_fusion.1), channel_id=1, source_target_pairs={{0,4},{1,2},{2,1},{3,7},{4,0},{5,6},{6,5},{7,3},{8,12},{9,10},{10,... | collective-permute-start | bytes 1179656 | tf_op jit(solution)/shard_map/ppermute | solution.py:44
  29.7 1.0 slice.69
  30.7 1.2 %slice_select_fusion.1 = bf16[256,1024]{1,0:T(8,128)(2,1)S(1)} fusion(bf16[256,1792]{1,0:T(8,128)(2,1)} %collective-permute-done, pred[]{:T(512)S(6)} %select_n.212), kind=kLoop, calls=%fused_computation.32 | loop fusion | flops 262144 | bytes 1048577 | tf_op jit(solution)/shard_map/jit(_where)/select_n | solution.py:100
  32.0 0.2 collective-permute-done.6
  32.2 1.3 %collective-permute-start.7 = (bf16[192,1024]{1,0:T(8,128)(2,1)S(1)}, bf16[192,1024]{1,0:T(8,128)(2,1)S(1)}, u32[]{:S(2)}, u32[]{:S(2)}) collective-permute-start(bf16[192,1024]{1,0:T(8,128)(2,1)S(1)} %collective-permute-done.6), channel_id=1, source_target_pairs={{0,4},{1,2},{2,1},{3,7},{4,0},{5,6},{6,5},{7,3},{8,12},{9,10},{10,... | collective-permute-start | bytes 1179656 | tf_op jit(solution)/shard_map/ppermute | solution.py:44
  33.5 1.0 slice.70
  34.5 1.2 %slice_select_fusion = bf16[256,1024]{1,0:T(8,128)(2,1)S(1)} fusion(bf16[256,1792]{1,0:T(8,128)(2,1)} %collective-permute-done.2, pred[]{:T(512)S(6)} %select_n.232), kind=kLoop, calls=%fused_computation.31 | loop fusion | flops 262144 | bytes 1048577 | tf_op jit(solution)/shard_map/jit(_where)/select_n | solution.py:101
  35.8 0.8 copy-done.4
  36.5 1.4 %convolution_convert_fusion.1 = bf16[768,1024]{1,0:T(8,128)(2,1)S(1)} fusion(bf16[256,1024]{1,0:T(8,128)(2,1)S(1)} %slice_select_fusion, bf16[256,1024]{1,0:T(8,128)(2,1)S(1)} %slice_select_fusion.1, bf16[256,1024]{1,0:T(8,128)(2,1)S(1)} %copy-done.6, bf16[256,768]{1,0:T(8,128)(2,1)S(1)} %slice.70, bf16[256,768]{1,0:T(8,128)(2,1)S(1)} %slice.69, ...), kind=kOutput, calls=%fused_computation.3 | convolution fusion | flops 1217003520 | bytes 4325376 | tf_op jit(solution)/shard_map/dot_general | solution.py:105
  38.0 0.1 constant_dynamic-slice_fusion
  38.1 0.8 broadcast_select_fusion.7
  38.9 2.7 %collective-permute-start.9 = (bf16[192,1024]{1,0:T(8,128)(2,1)}, bf16[192,1024]{1,0:T(8,128)(2,1)}, u32[]{:S(2)}, u32[]{:S(2)}) collective-permute-start(bf16[192,1024]{1,0:T(8,128)(2,1)} %broadcast_select_fusion.7), channel_id=1, source_target_pairs={{0,1},{1,0},{2,3},{3,2},{4,5},{5,4},{6,7},{7,6},{8,9},{9,8},{10,11... | collective-permute-start | bytes 1179656 | tf_op jit(solution)/shard_map/ppermute | solution.py:41
  41.7 2.6 %collective-permute-done.7 = bf16[192,1024]{1,0:T(8,128)(2,1)S(1)} collective-permute-done((bf16[192,1024]{1,0:T(8,128)(2,1)S(1)}, bf16[192,1024]{1,0:T(8,128)(2,1)S(1)}, u32[]{:S(2)}, u32[]{:S(2)}) %collective-permute-start.7) | collective-permute-done | bytes 393248 | tf_op jit(solution)/shard_map/ppermute | solution.py:44
  44.2 0.7 copy-done.1
  45.0 0.8 broadcast_select_fusion.9
  45.8 2.5 %collective-permute-done.9 = bf16[192,1024]{1,0:T(8,128)(2,1)} collective-permute-done((bf16[192,1024]{1,0:T(8,128)(2,1)}, bf16[192,1024]{1,0:T(8,128)(2,1)}, u32[]{:S(2)}, u32[]{:S(2)}) %collective-permute-start.9) | collective-permute-done | bytes 393248 | tf_op jit(solution)/shard_map/ppermute | solution.py:41
  48.3 8.8 %collective-permute-done.8 = bf16[192,1024]{1,0:T(8,128)(2,1)S(1)} collective-permute-done((bf16[192,1024]{1,0:T(8,128)(2,1)}, bf16[192,1024]{1,0:T(8,128)(2,1)S(1)}, u32[]{:S(2)}, u32[]{:S(2)}) %collective-permute-start.8) | collective-permute-done | bytes 393248 | tf_op jit(solution)/shard_map/ppermute | solution.py:41
  57.1 1.1 broadcast_select_fusion.17
  58.3 0.2 broadcast_select_fusion.16
  58.5 0.8 copy-done.9
  59.2 0.1 copy-done.11
  59.4 1.4 %convolution_convert_fusion = bf16[768,1024]{1,0:T(8,128)(2,1)S(1)} fusion(bf16[256,768]{1,0:T(8,128)(2,1)S(1)} %copy-done.11, bf16[256,768]{1,0:T(8,128)(2,1)S(1)} %copy-done.9, bf16[256,768]{1,0:T(8,128)(2,1)S(1)} %bitcast_select_fusion.3, bf16[192,1024]{1,0:T(8,128)(2,1)S(1)} %get-tuple-element.22, bf16[192,1024]{1,0:T(8,128)(2,1)S(1)} %get-tuple-element.21, ...), kind=kOutput, calls=%fused_computation.2 | convolution fusion | flops 1218576384 | bytes 4325376 | tf_op jit(solution)/shard_map/dot_general | solution.py:133
  60.8 1.4 %fusion.6 = f32[768,768]{1,0:T(8,128)S(1)} fusion(bf16[256,1024]{1,0:T(8,128)(2,1)S(1)} %copy-done.5, bf16[256,1024]{1,0:T(8,128)(2,1)S(1)} %copy-done.3, bf16[256,1024]{1,0:T(8,128)(2,1)S(1)} %copy-done.7, bf16[192,1024]{1,0:T(8,128)(2,1)S(1)} %get-tuple-element.22, bf16[192,1024]{1,0:T(8,128)(2,1)S(1)} %get-tuple-element.21, ...), kind=kOutput, calls=%fused_computation.29 | convolution fusion | flops 1218969600 | bytes 5505024 | tf_op jit(solution)/shard_map/dot_general | solution.py:134
  62.2 1.1 add_convert_fusion.2
  63.4 2.2 %collective-permute-start.12 = (bf16[192,1024]{1,0:T(8,128)(2,1)S(1)}, bf16[192,1024]{1,0:T(8,128)(2,1)S(1)}, u32[]{:S(2)}, u32[]{:S(2)}) collective-permute-start(bf16[192,1024]{1,0:T(8,128)(2,1)S(1)} %add_convert_fusion.2), channel_id=1, source_target_pairs={{0,4},{1,2},{2,1},{3,7},{4,0},{5,6},{6,5},{7,3},{8,12},{9,10},{10,... | collective-permute-start | bytes 1179656 | tf_op jit(solution)/shard_map/ppermute | solution.py:44
  65.5 0.1 slice.100
  65.7 0.1 pad_maximum_fusion.3
  65.8 0.7 collective-permute-start.11
  66.6 9.3 %collective-permute-start.10 = (bf16[256,1792]{1,0:T(8,128)(2,1)S(1)}, bf16[256,1792]{1,0:T(8,128)(2,1)S(1)}, u32[]{:S(2)}, u32[]{:S(2)}) collective-permute-start(bf16[256,1792]{1,0:T(8,128)(2,1)S(1)} %get-tuple-element.19), channel_id=1, source_target_pairs={{0,4},{4,0},{8,12},{12,8},{16,20},{20,16},{24,28},{28,24},{1,5},{5... | collective-permute-start | bytes 2752520 | tf_op jit(solution)/shard_map/ppermute | solution.py:35
  75.9 0.1 add_convert_fusion
  76.0 1.1 collective-permute-start.14
  77.1 0.1 fusion.7
  78.5 8.2 %collective-permute-done.14 = bf16[192,1024]{1,0:T(8,128)(2,1)S(1)} collective-permute-done((bf16[192,1024]{1,0:T(8,128)(2,1)S(1)}, bf16[192,1024]{1,0:T(8,128)(2,1)S(1)}, u32[]{:S(2)}, u32[]{:S(2)}) %collective-permute-start.14) | collective-permute-done | bytes 393248 | tf_op jit(solution)/shard_map/ppermute | solution.py:44
  86.7 0.9 collective-permute-done.13
  87.7 0.2 fusion.8
  87.9 5.0 %collective-permute-start.16 = (bf16[192,1024]{1,0:T(8,128)(2,1)S(1)}, bf16[192,1024]{1,0:T(8,128)(2,1)S(1)}, u32[]{:S(2)}, u32[]{:S(2)}) collective-permute-start(bf16[192,1024]{1,0:T(8,128)(2,1)S(1)} %fusion.8), channel_id=1, source_target_pairs={{8,0},{12,4},{16,8},{20,12},{24,16},{28,20},{9,1},{13,5},{17,9},{2... | collective-permute-start | bytes 1179656 | tf_op jit(solution)/shard_map/ppermute | solution.py:38
  92.8 1.3 %collective-permute-start.15 = (bf16[192,1024]{1,0:T(8,128)(2,1)S(1)}, bf16[192,1024]{1,0:T(8,128)(2,1)S(1)}, u32[]{:S(2)}, u32[]{:S(2)}) collective-permute-start(bf16[192,1024]{1,0:T(8,128)(2,1)S(1)} %fusion.8), channel_id=1, source_target_pairs={{0,8},{4,12},{8,16},{12,20},{16,24},{20,28},{1,9},{5,13},{9,17},{1... | collective-permute-start | bytes 1179656 | tf_op jit(solution)/shard_map/ppermute | solution.py:38
  94.2 0.1 broadcast_select_fusion.1
  94.3 0.1 broadcast_select_fusion.3
  94.4 3.6 %collective-permute-done.16 = bf16[192,1024]{1,0:T(8,128)(2,1)S(1)} collective-permute-done((bf16[192,1024]{1,0:T(8,128)(2,1)S(1)}, bf16[192,1024]{1,0:T(8,128)(2,1)S(1)}, u32[]{:S(2)}, u32[]{:S(2)}) %collective-permute-start.16) | collective-permute-done | bytes 393248 | tf_op jit(solution)/shard_map/ppermute | solution.py:38
  98.0 9.5 %collective-permute-done.15 = bf16[192,1024]{1,0:T(8,128)(2,1)S(1)} collective-permute-done((bf16[192,1024]{1,0:T(8,128)(2,1)S(1)}, bf16[192,1024]{1,0:T(8,128)(2,1)S(1)}, u32[]{:S(2)}, u32[]{:S(2)}) %collective-permute-start.15) | collective-permute-done | bytes 393248 | tf_op jit(solution)/shard_map/ppermute | solution.py:38
  107.4 0.4 fusion.10
  107.8 4.0 %collective-permute-start.17 = (bf16[192,1024]{1,0:T(8,128)(2,1)S(1)}, bf16[192,1024]{1,0:T(8,128)(2,1)S(1)}, u32[]{:S(2)}, u32[]{:S(2)}) collective-permute-start(bf16[192,1024]{1,0:T(8,128)(2,1)S(1)} %get-tuple-element.11), channel_id=1, source_target_pairs={{0,4},{4,0},{8,12},{12,8},{16,20},{20,16},{24,28},{28,24},{1,5},{5... | collective-permute-start | bytes 1179656 | tf_op jit(solution)/shard_map/ppermute | solution.py:35
  111.8 1.1 maximum_bitcast_fusion
  112.9 0.8 fusion.9
  113.7 0.9 maximum_bitcast_fusion.1
  (40 shorter events, 0.3 us)
Async XLA Ops:
  3.8 2.6 %copy-start = (bf16[1,192,2048]{2,1,0:T(8,128)(2,1)S(1)}, bf16[1,192,2048]{2,1,0:T(8,128)(2,1)}, u32[]{:S(2)}) copy-start(bf16[1,192,2048]{2,1,0:T(8,128)(2,1)} %param.8) | copy-start | bytes 2359300
  4.7 3.2 %copy-start.12 = (s32[8]{0:T(128)S(1)}, s32[8]{0:T(128)}, u32[]{:S(2)}) copy-start(s32[8]{0:T(128)} %param.9) | copy-start | bytes 100
  4.7 6.5 %copy-start.13 = (s32[2]{0:T(128)S(1)}, s32[2]{0:T(128)}, u32[]{:S(2)}) copy-start(s32[2]{0:T(128)} %constant.57.clone) | copy-start | bytes 28
  5.7 7.6 %collective-permute-start.1 = (bf16[256,1792]{1,0:T(8,128)(2,1)}, bf16[256,1792]{1,0:T(8,128)(2,1)S(1)}, u32[]{:S(2)}, u32[]{:S(2)}) collective-permute-start(bf16[256,1792]{1,0:T(8,128)(2,1)} %pad_maximum_fusion.4), channel_id=1, source_target_pairs={{12,24},{16,4},{13,25},{17,5},{14,26},{18,6},{15,27},{19,7}} | collective-permute-start | bytes 2752520 | tf_op jit(solution)/shard_map/ppermute | solution.py:38
  6.4 5.4 %collective-permute-start.3 = (bf16[192,1024]{1,0:T(8,128)(2,1)S(1)}, bf16[192,1024]{1,0:T(8,128)(2,1)S(1)}, u32[]{:S(2)}, u32[]{:S(2)}) collective-permute-start(bf16[192,1024]{1,0:T(8,128)(2,1)S(1)} %dynamic-slice_bitcast_fusion), channel_id=1, source_target_pairs={{0,4},{4,0},{8,12},{12,8},{16,20},{20,16},{24,28},{28,24},{1,5},{5... | collective-permute-start | bytes 1179656 | tf_op jit(solution)/shard_map/ppermute | solution.py:35
  7.8 21.9 %collective-permute-start = (bf16[256,1792]{1,0:T(8,128)(2,1)}, bf16[256,1792]{1,0:T(8,128)(2,1)}, u32[]{:S(2)}, u32[]{:S(2)}) collective-permute-start(bf16[256,1792]{1,0:T(8,128)(2,1)} %pad_maximum_fusion.4), channel_id=1, source_target_pairs={{0,4},{4,0},{8,12},{12,8},{16,20},{20,16},{24,28},{28,24},{1,5},{5... | collective-permute-start | bytes 2752520 | tf_op jit(solution)/shard_map/ppermute | solution.py:35
  12.0 12.2 %collective-permute-start.4 = (bf16[192,1024]{1,0:T(8,128)(2,1)S(1)}, bf16[192,1024]{1,0:T(8,128)(2,1)}, u32[]{:S(2)}, u32[]{:S(2)}) collective-permute-start(bf16[192,1024]{1,0:T(8,128)(2,1)S(1)} %bitcast_select_fusion.2), channel_id=1, source_target_pairs={{0,8},{4,12},{8,16},{12,20},{16,24},{20,28},{1,9},{5,13},{9,17},{1... | collective-permute-start | bytes 1179656 | tf_op jit(solution)/shard_map/ppermute | solution.py:38
  15.1 18.4 %collective-permute-start.2 = (bf16[256,1792]{1,0:T(8,128)(2,1)}, bf16[256,1792]{1,0:T(8,128)(2,1)}, u32[]{:S(2)}, u32[]{:S(2)}) collective-permute-start(bf16[256,1792]{1,0:T(8,128)(2,1)} %broadcast_select_fusion), channel_id=1, source_target_pairs={{24,16},{4,12},{8,4},{20,24},{25,17},{5,13},{9,5},{21,25},{26,18},... | collective-permute-start | bytes 2752520 | tf_op jit(solution)/shard_map/ppermute | solution.py:38
  24.4 7.8 %collective-permute-start.6 = (bf16[192,1024]{1,0:T(8,128)(2,1)S(1)}, bf16[192,1024]{1,0:T(8,128)(2,1)S(1)}, u32[]{:S(2)}, u32[]{:S(2)}) collective-permute-start(bf16[192,1024]{1,0:T(8,128)(2,1)S(1)} %bitcast_select_fusion.1), channel_id=1, source_target_pairs={{0,1},{1,0},{2,3},{3,2},{4,5},{5,4},{6,7},{7,6},{8,9},{9,8},{10,11... | collective-permute-start | bytes 1179656 | tf_op jit(solution)/shard_map/ppermute | solution.py:41
  27.2 9.4 %copy-start.6 = (bf16[256,1024]{1,0:T(8,128)(2,1)S(1)}, bf16[256,1024]{1,0:T(8,128)(2,1)}, u32[]{:S(2)}) copy-start(bf16[256,1024]{1,0:T(8,128)(2,1)} %get-tuple-element.27) | copy-start | bytes 1572868
  27.2 10.9 %collective-permute-start.5 = (bf16[192,1024]{1,0:T(8,128)(2,1)S(1)}, bf16[192,1024]{1,0:T(8,128)(2,1)S(1)}, u32[]{:S(2)}, u32[]{:S(2)}) collective-permute-start(bf16[192,1024]{1,0:T(8,128)(2,1)S(1)} %bitcast_select_fusion.1), channel_id=1, source_target_pairs={{0,4},{1,2},{2,1},{3,7},{4,0},{5,6},{6,5},{7,3},{8,12},{9,10},{10,... | collective-permute-start | bytes 1179656 | tf_op jit(solution)/shard_map/ppermute | solution.py:44
  30.7 7.3 %copy-start.8 = (bf16[256,768]{1,0:T(8,128)(2,1)}, bf16[256,768]{1,0:T(8,128)(2,1)S(1)}, u32[]{:S(2)}) copy-start(bf16[256,768]{1,0:T(8,128)(2,1)S(1)} %slice.69) | copy-start | bytes 1179652
  32.0 3.8 %copy-start.2 = (bf16[256,1024]{1,0:T(8,128)(2,1)}, bf16[256,1024]{1,0:T(8,128)(2,1)S(1)}, u32[]{:S(2)}) copy-start(bf16[256,1024]{1,0:T(8,128)(2,1)S(1)} %slice_select_fusion.1) | copy-start | bytes 1572868
  32.2 12.1 %collective-permute-start.7 = (bf16[192,1024]{1,0:T(8,128)(2,1)S(1)}, bf16[192,1024]{1,0:T(8,128)(2,1)S(1)}, u32[]{:S(2)}, u32[]{:S(2)}) collective-permute-start(bf16[192,1024]{1,0:T(8,128)(2,1)S(1)} %collective-permute-done.6), channel_id=1, source_target_pairs={{0,4},{1,2},{2,1},{3,7},{4,0},{5,6},{6,5},{7,3},{8,12},{9,10},{10,... | collective-permute-start | bytes 1179656 | tf_op jit(solution)/shard_map/ppermute | solution.py:44
  34.5 3.5 %copy-start.10 = (bf16[256,768]{1,0:T(8,128)(2,1)}, bf16[256,768]{1,0:T(8,128)(2,1)S(1)}, u32[]{:S(2)}) copy-start(bf16[256,768]{1,0:T(8,128)(2,1)S(1)} %slice.70) | copy-start | bytes 1179652
  35.7 0.8 copy-start.4
  38.9 9.3 %collective-permute-start.9 = (bf16[192,1024]{1,0:T(8,128)(2,1)}, bf16[192,1024]{1,0:T(8,128)(2,1)}, u32[]{:S(2)}, u32[]{:S(2)}) collective-permute-start(bf16[192,1024]{1,0:T(8,128)(2,1)} %broadcast_select_fusion.7), channel_id=1, source_target_pairs={{0,1},{1,0},{2,3},{3,2},{4,5},{5,4},{6,7},{7,6},{8,9},{9,8},{10,11... | collective-permute-start | bytes 1179656 | tf_op jit(solution)/shard_map/ppermute | solution.py:41
  44.2 0.7 copy-start.1
  45.8 11.3 %collective-permute-start.8 = (bf16[192,1024]{1,0:T(8,128)(2,1)}, bf16[192,1024]{1,0:T(8,128)(2,1)S(1)}, u32[]{:S(2)}, u32[]{:S(2)}) collective-permute-start(bf16[192,1024]{1,0:T(8,128)(2,1)} %broadcast_select_fusion.9), channel_id=1, source_target_pairs={{0,1},{1,0},{2,3},{3,2},{4,5},{5,4},{6,7},{7,6},{8,9},{9,8},{10,11... | collective-permute-start | bytes 1179656 | tf_op jit(solution)/shard_map/ppermute | solution.py:41
  58.2 1.0 copy-start.9
  58.2 1.1 copy-start.11
  59.3 1.4 %copy-start.3 = (bf16[256,1024]{1,0:T(8,128)(2,1)S(1)}, bf16[256,1024]{1,0:T(8,128)(2,1)}, u32[]{:S(2)}) copy-start(bf16[256,1024]{1,0:T(8,128)(2,1)} %copy-done.2) | copy-start | bytes 1572868
  59.4 1.4 %copy-start.5 = (bf16[256,1024]{1,0:T(8,128)(2,1)S(1)}, bf16[256,1024]{1,0:T(8,128)(2,1)}, u32[]{:S(2)}) copy-start(bf16[256,1024]{1,0:T(8,128)(2,1)} %copy-done.4) | copy-start | bytes 1572868
  59.4 1.4 %copy-start.7 = (bf16[256,1024]{1,0:T(8,128)(2,1)S(1)}, bf16[256,1024]{1,0:T(8,128)(2,1)}, u32[]{:S(2)}) copy-start(bf16[256,1024]{1,0:T(8,128)(2,1)} %get-tuple-element.27) | copy-start | bytes 1572868
  63.4 13.7 %collective-permute-start.12 = (bf16[192,1024]{1,0:T(8,128)(2,1)S(1)}, bf16[192,1024]{1,0:T(8,128)(2,1)S(1)}, u32[]{:S(2)}, u32[]{:S(2)}) collective-permute-start(bf16[192,1024]{1,0:T(8,128)(2,1)S(1)} %add_convert_fusion.2), channel_id=1, source_target_pairs={{0,4},{1,2},{2,1},{3,7},{4,0},{5,6},{6,5},{7,3},{8,12},{9,10},{10,... | collective-permute-start | bytes 1179656 | tf_op jit(solution)/shard_map/ppermute | solution.py:44
  65.8 28.3 %collective-permute-start.11 = (bf16[256,1792]{1,0:T(8,128)(2,1)S(1)}, bf16[256,1792]{1,0:T(8,128)(2,1)S(1)}, u32[]{:S(2)}, u32[]{:S(2)}) collective-permute-start(bf16[256,1792]{1,0:T(8,128)(2,1)S(1)} %get-tuple-element.18), channel_id=1, source_target_pairs={{4,8},{16,12},{12,16},{24,20},{5,9},{17,13},{13,17},{25,21},{6,10}... | collective-permute-start | bytes 2752520 | tf_op jit(solution)/shard_map/ppermute | solution.py:38
  66.6 27.6 %collective-permute-start.10 = (bf16[256,1792]{1,0:T(8,128)(2,1)S(1)}, bf16[256,1792]{1,0:T(8,128)(2,1)S(1)}, u32[]{:S(2)}, u32[]{:S(2)}) collective-permute-start(bf16[256,1792]{1,0:T(8,128)(2,1)S(1)} %get-tuple-element.19), channel_id=1, source_target_pairs={{0,4},{4,0},{8,12},{12,8},{16,20},{20,16},{24,28},{28,24},{1,5},{5... | collective-permute-start | bytes 2752520 | tf_op jit(solution)/shard_map/ppermute | solution.py:35
  76.0 10.7 %collective-permute-start.14 = (bf16[192,1024]{1,0:T(8,128)(2,1)S(1)}, bf16[192,1024]{1,0:T(8,128)(2,1)S(1)}, u32[]{:S(2)}, u32[]{:S(2)}) collective-permute-start(bf16[192,1024]{1,0:T(8,128)(2,1)S(1)} %add_convert_fusion), channel_id=1, source_target_pairs={{0,4},{1,2},{2,1},{3,7},{4,0},{5,6},{6,5},{7,3},{8,12},{9,10},{10,... | collective-permute-start | bytes 1179656 | tf_op jit(solution)/shard_map/ppermute | solution.py:44
  77.2 10.4 %collective-permute-start.13 = (bf16[192,1024]{1,0:T(8,128)(2,1)S(1)}, bf16[192,1024]{1,0:T(8,128)(2,1)S(1)}, u32[]{:S(2)}, u32[]{:S(2)}) collective-permute-start(bf16[192,1024]{1,0:T(8,128)(2,1)S(1)} %fusion.7), channel_id=1, source_target_pairs={{0,1},{1,0},{2,3},{3,2},{4,5},{5,4},{6,7},{7,6},{8,9},{9,8},{10,11... | collective-permute-start | bytes 1179656 | tf_op jit(solution)/shard_map/ppermute | solution.py:41
  87.9 10.1 %collective-permute-start.16 = (bf16[192,1024]{1,0:T(8,128)(2,1)S(1)}, bf16[192,1024]{1,0:T(8,128)(2,1)S(1)}, u32[]{:S(2)}, u32[]{:S(2)}) collective-permute-start(bf16[192,1024]{1,0:T(8,128)(2,1)S(1)} %fusion.8), channel_id=1, source_target_pairs={{8,0},{12,4},{16,8},{20,12},{24,16},{28,20},{9,1},{13,5},{17,9},{2... | collective-permute-start | bytes 1179656 | tf_op jit(solution)/shard_map/ppermute | solution.py:38
  92.8 14.6 %collective-permute-start.15 = (bf16[192,1024]{1,0:T(8,128)(2,1)S(1)}, bf16[192,1024]{1,0:T(8,128)(2,1)S(1)}, u32[]{:S(2)}, u32[]{:S(2)}) collective-permute-start(bf16[192,1024]{1,0:T(8,128)(2,1)S(1)} %fusion.8), channel_id=1, source_target_pairs={{0,8},{4,12},{8,16},{12,20},{16,24},{20,28},{1,9},{5,13},{9,17},{1... | collective-permute-start | bytes 1179656 | tf_op jit(solution)/shard_map/ppermute | solution.py:38
  107.8 5.8 %collective-permute-start.17 = (bf16[192,1024]{1,0:T(8,128)(2,1)S(1)}, bf16[192,1024]{1,0:T(8,128)(2,1)S(1)}, u32[]{:S(2)}, u32[]{:S(2)}) collective-permute-start(bf16[192,1024]{1,0:T(8,128)(2,1)S(1)} %get-tuple-element.11), channel_id=1, source_target_pairs={{0,4},{4,0},{8,12},{12,8},{16,20},{20,16},{24,28},{28,24},{1,5},{5... | collective-permute-start | bytes 1179656 | tf_op jit(solution)/shard_map/ppermute | solution.py:35

commit v3 on v1

v3 whole, which is shorter than its diff:
```python
import jax
import jax.numpy as jnp
from jax import lax
from jax.experimental import pallas as pl
from jax.experimental.pallas import tpu as pltpu
from jax.sharding import PartitionSpec as P


BF16 = jnp.bfloat16
F32 = jnp.float32
BLOCK = 128
FLAGS = (
    "odd", "z", "count", "partner", "helps", "begins", "before_two",
    "after_two", "export_own", "far_weight", "far_grad", "relay", "by_one",
)


def local_kernel(kernel, out_shapes, scratch=(), flops=0, moved=0, mib=8):
    def call(flags, *arrays):
        vmem = pl.BlockSpec(memory_space=pltpu.VMEM)
        return pl.pallas_call(
            kernel,
            out_shape=out_shapes,
            in_specs=[pl.BlockSpec(memory_space=pltpu.SMEM)] + [vmem] * len(arrays),
            out_specs=jax.tree.map(lambda _: vmem, out_shapes),
            scratch_shapes=list(scratch),
            compiler_params=pltpu.CompilerParams(vmem_limit_bytes=mib << 20),
            cost_estimate=pl.CostEstimate(
                flops=flops, bytes_accessed=moved, transcendentals=0
            ),
        )(flags, *arrays)

    return call


def flag(ref, name):
    return ref[FLAGS.index(name)]


def cols(at, size):
    return pl.ds(pl.multiple_of(at, BLOCK), size)


def copy_live(flags, rows, store):
    for r in range(0, rows, BLOCK):
        store(slice(r, r + BLOCK), r < flag(flags, "count"))


def masked(keep, x):
    return jnp.where(keep, x, jnp.zeros_like(x))


def pack_kernel(flags, hid, cot, sent_h, sent_c):
    half = cot.shape[1] // 2
    other = cols((1 - flag(flags, "odd")) * half, half)

    def store(r, live):
        sent_h[r, :] = masked(live, hid[r, :])
        sent_c[r, :] = masked(live, cot[r, other])

    copy_live(flags, hid.shape[0], store)


def choose_kernel(name):
    def kernel(flags, yes, no, out):
        @pl.when(flag(flags, name) != 0)
        def _():
            out[...] = yes[...]

        @pl.when(flag(flags, name) == 0)
        def _():
            out[...] = no[...]

    return kernel


def export_kernel(flags, stored, partner_part, out):
    half = out.shape[1]

    @pl.when(flag(flags, "export_own") != 0)
    def _():
        out[...] = stored[:, cols(flag(flags, "odd") * half, half)]

    @pl.when(flag(flags, "export_own") == 0)
    def _():
        out[...] = partner_part[...]


def unit_kernel(flags, stored, partner_part, came, out):
    half = out.shape[1]
    begins = flag(flags, "begins") != 0
    paired = (flag(flags, "odd") != 0) & (flag(flags, "before_two") == 0)

    @pl.when(begins)
    def _():
        out[...] = stored[:, cols(flag(flags, "odd") * half, half)]

    @pl.when(jnp.logical_not(begins) & paired)
    def _():
        out[...] = partner_part[...]

    @pl.when(jnp.logical_not(begins | paired))
    def _():
        out[...] = came[...]


def grad_kernel(flags, hid, cot, core_h, core_c, near_h, near_c, t0, t1, t2, t3, ht, cs):
    rows, units = hid.shape
    half = cot.shape[1] // 2
    own = cols(flag(flags, "odd") * half, half)

    def store(r, live):
        cs[r, :] = masked(live, cot[r, own])

    copy_live(flags, rows, store)
    cs[rows : 2 * rows, :] = masked(flag(flags, "partner") != 0, core_c[...])
    cs[2 * rows :, :] = masked(flag(flags, "helps") != 0, near_c[...])
    ht[:, :rows] = hid[...].T
    ht[:, rows : 2 * rows] = core_h[...].T
    ht[:, 2 * rows :] = near_h[...].T
    z = flag(flags, "z")
    quarter = units // 4
    for k, term in enumerate((t0, t1, t2, t3)):
        at = pl.multiple_of((z ^ k) * quarter, 16)
        term[...] = jnp.dot(
            ht[pl.ds(at, quarter), :], cs[...], preferred_element_type=F32
        ).astype(BF16)


def sum_kernel(flags, held, left, right, *rest):
    far, own, other = rest[:-2], rest[-2], rest[-1]
    none = jnp.zeros((), F32)

    def add(x, keep):
        return jnp.where(keep, x[...].astype(F32), none)

    total = held[...].astype(F32) + add(left, flag(flags, "before_two") != 0)
    own[...] = (total + add(right, flag(flags, "after_two") != 0)).astype(BF16)

    @pl.when(flag(flags, "partner") != 0)
    def _():
        other[...] = own[...]

    @pl.when(flag(flags, "partner") == 0)
    def _():
        odd = flag(flags, "odd") != 0
        theirs = jnp.where(odd, left[...].astype(F32), right[...].astype(F32))
        if far:
            more = jnp.where(odd, far[0][...].astype(F32), far[1][...].astype(F32))
            theirs = theirs + jnp.where(flag(flags, "far_grad") != 0, more, none)
        other[...] = theirs.astype(BF16)


def forward_kernel(flags, hid, cot, core_h, core_c, near_h, near_c, u, a1, m1, a2, m2, a3,
                   out, hg, to_core, to_near, weight):
    rows, units = hid.shape
    half = cot.shape[1] // 2
    z = flag(flags, "z")
    middle = (z == 1) | (z == 2)
    quarter = units // 4

    def place(k, value):
        at = pl.multiple_of((z ^ k) * quarter, 16)
        weight[pl.ds(at, quarter), :] = value

    place(0, u[...])
    place(1, a1[...])

    @pl.when(middle)
    def _():
        place(2, m2[...])
        place(3, m1[...])

    @pl.when(jnp.logical_not(middle))
    def _():
        place(2, a2[...])
        place(3, a3[...])

    own = cols(flag(flags, "odd") * half, half)
    w = weight[...]

    def products(h, c):
        o = jnp.dot(h, w, preferred_element_type=F32)
        g = lax.dot_general(c, w, (((1,), (1,)), ((), ())), preferred_element_type=F32)
        return o, g

    def own_rows(r, live):
        o, g = products(masked(live, hid[r, :]), masked(live, cot[r, own]))
        out[r, :] = o.astype(BF16)
        hg[r, :] = g

    copy_live(flags, rows, own_rows)
    for h, c, dst in ((core_h, core_c, to_core), (near_h, near_c, to_near)):
        o, g = products(h[...], c[...])
        dst[:, :half] = o.astype(BF16)
        dst[:, half:] = g.astype(BF16)


def output_kernel(flags, out, hg, core, near, output, hidden_grad):
    half = out.shape[1]
    odd = flag(flags, "odd")
    output[:, cols(odd * half, half)] = out[...]

    def finish(back):
        output[:, cols((1 - odd) * half, half)] = back[:, :half]
        hidden_grad[...] = (hg[...] + back[:, half:].astype(F32)).astype(BF16)

    @pl.when(flag(flags, "partner") != 0)
    def _():
        finish(core)

    @pl.when(flag(flags, "partner") == 0)
    def _():
        finish(near)


def join_kernel(flags, own, other, whole):
    half = own.shape[1]
    odd = flag(flags, "odd")
    whole[:, cols(odd * half, half)] = own[...]
    whole[:, cols((1 - odd) * half, half)] = other[...]


def make_body(n_ep, n_dp):
    assert n_dp == 4 and n_ep % 2 == 0
    both = ("ep", "dp")
    core_pairs = [(s, s ^ 1) for s in range(n_ep)]
    help_pairs = [(s, s + 1 if s % 2 else s - 1) for s in range(2, n_ep - 2)]
    back_pairs = [(b, a) for a, b in help_pairs]
    far = [(a, b) for a, b in help_pairs if {a % 8, b % 8} == {3, 4}]
    relays = {a ^ 5 for a, b in far}
    near = [(a, b) for a, b in help_pairs if (a, b) not in far]
    hop_one = [(a, a ^ 5) for a, b in far] + [p for p in near if p[0] in relays]
    hop_two = [(a ^ 5, b) for a, b in far] + [p for p in near if p[0] not in relays]
    by_one = {b for a, b in near if a in relays}
    right_two = [(s, s + 2) for s in range(n_ep - 2)]
    left_two = [(s + 2, s) for s in range(n_ep - 2)]
    right_four_weight = [(s - 4, s) for s in range(6, n_ep - 2, 2)]
    right_four_grad = [(s - 4, s) for s in range(7, n_ep - 2, 2)]
    left_four_grad = [(s + 4, s) for s in range(2, n_ep - 7, 2)]
    side_pairs = [(0, 1), (1, 0), (2, 3), (3, 2)]
    middle_pairs = []
    for s in range(n_ep):
        for z in range(n_dp):
            t, w = (s, z ^ 3) if z in (1, 2) else (s ^ 1, z)
            middle_pairs.append((s * n_dp + z, t * n_dp + w))

    def permute(x, axes, pairs):
        return lax.ppermute(x, axes, pairs) if pairs else jnp.zeros_like(x)

    def core(x):
        return permute(x, "ep", core_pairs)

    def shift(x, pairs):
        return permute(x, "ep", pairs)

    def side(x):
        return permute(x, "dp", side_pairs)

    def middle(x):
        return permute(x, both, middle_pairs)

    def plus(a, b):
        return (a.astype(F32) + b.astype(F32)).astype(BF16)

    def make_flags(slot_expert, count, s, z):
        places = lax.iota(jnp.int32, n_ep)
        odd = places % 2 == 1
        padded = jnp.pad(slot_expert, 4, constant_values=-1)
        e = {d: padded[4 + d : 4 + d + n_ep] for d in range(-4, 5)}
        eq = {d: e[d] == e[0] for d in e}
        partner = jnp.where(odd, eq[-1], eq[1])

        def among(members):
            found = places < 0
            for m in sorted(members):
                found = found | (places == m)
            return found

        rows = {
            "odd": odd,
            "z": z + 0 * places,
            "count": count + 0 * places,
            "partner": partner,
            "helps": jnp.where(odd, eq[1] & ~eq[2], eq[-1] & ~eq[-2]),
            "begins": ~eq[-1],
            "before_two": eq[-2],
            "after_two": eq[2],
            "export_own": partner != odd,
            "far_weight": eq[-3] & ~odd,
            "far_grad": jnp.where(odd, e[-4] == e[-1], e[4] == e[1]),
            "relay": among(relays),
            "by_one": among(by_one),
        }
        table = jnp.stack([rows[name].astype(jnp.int32) for name in FLAGS])
        return jnp.sum(jnp.where(places == s, table, 0), axis=1)

    def compute(hidden, cotangent, down_weight, slot_expert, row_counts):
        s = lax.axis_index("ep")
        z = lax.axis_index("dp")
        is_middle = (z == 1) | (z == 2)
        hid, cot, stored = hidden[0], cotangent[0], down_weight[0]
        capacity, units = hid.shape
        quarter, features = stored.shape
        half = features // 2
        flags = make_flags(slot_expert, row_counts[0, 0], s, z)

        def is_set(name):
            return flags[FLAGS.index(name)] != 0

        own_at = (s % 2) * half

        other_part = lax.dynamic_slice(stored, (0, half - own_at), (quarter, half))
        other_part, hid, cot = lax.optimization_barrier((other_part, hid, cot))
        own_part = lax.dynamic_slice(stored, (0, own_at), (quarter, half))
        piece = jax.ShapeDtypeStruct((quarter, half), BF16)
        h_piece = jax.ShapeDtypeStruct((capacity, units), BF16)
        c_piece = jax.ShapeDtypeStruct((capacity, half), BF16)
        packed = jax.ShapeDtypeStruct((capacity, units + half), BF16)
        wide = units + half
        small = 6 * quarter * half

        partner_part = core(other_part)
        export = local_kernel(export_kernel, piece, moved=small)(
            flags, stored, partner_part
        )
        came = shift(export, right_two)
        if right_four_weight:
            more = shift(export, right_four_weight)
            came = jnp.where(is_set("far_weight"), more, came)
        unit = local_kernel(unit_kernel, piece, moved=small)(
            flags, stored, partner_part, came
        )

        sent_h, sent_c = local_kernel(
            pack_kernel, [h_piece, c_piece], moved=4 * capacity * wide
        )(flags, hid, cot)

        def to_neighbour(x):
            first = shift(x, hop_one)
            passed = local_kernel(choose_kernel("relay"), x, moved=4 * x.size)(
                flags, first, x
            )
            arrived = shift(passed, hop_two)
            if by_one:
                arrived = jnp.where(is_set("by_one"), first, arrived)
            return arrived

        near = [to_neighbour(sent_h), to_neighbour(sent_c)]
        from_core = [core(sent_h), core(sent_c)]
        terms = local_kernel(
            grad_kernel,
            [piece] * 4,
            [
                pltpu.VMEM((units, 3 * capacity), BF16),
                pltpu.VMEM((3 * capacity, half), BF16),
            ],
            flops=6 * capacity * units * half,
            moved=2 * units * half + 6 * capacity * wide,
            mib=16,
        )(flags, hid, cot, *from_core, *near)

        a1 = side(unit)
        m1 = middle(unit)
        a2 = side(jnp.where(is_middle, m1, terms[3]))
        m2 = middle(a1)
        a3 = side(jnp.where(is_middle, m2, terms[2]))
        m3 = middle(plus(a2, terms[2]))
        last_side = jnp.where(is_middle, plus(m3, terms[1]), terms[1])
        last_middle = plus(a3, terms[3])
        last_side, last_middle, unit = lax.optimization_barrier(
            (last_side, last_middle, unit)
        )
        a4 = side(last_side)
        m4 = middle(last_middle)

        out, hg, to_core, to_next = local_kernel(
            forward_kernel,
            [
                jax.ShapeDtypeStruct((capacity, half), BF16),
                jax.ShapeDtypeStruct((capacity, units), F32),
                packed,
                packed,
            ],
            [pltpu.VMEM((units, half), BF16)],
            flops=12 * capacity * units * half,
            moved=2 * units * half + 12 * capacity * wide,
            mib=24,
        )(flags, hid, cot, *from_core, *near, unit, a1, m1, a2, m2, a3)
        a4, m4, to_core, to_next = lax.optimization_barrier((a4, m4, to_core, to_next))
        output, hidden_grad = local_kernel(
            output_kernel,
            [
                jax.ShapeDtypeStruct((capacity, features), BF16),
                jax.ShapeDtypeStruct((capacity, units), BF16),
            ],
            moved=8 * capacity * wide,
        )(flags, out, hg, core(to_core), shift(to_next, back_pairs))

        total = a4.astype(F32) + terms[0].astype(F32)
        total = total + jnp.where(is_middle, m4.astype(F32), 0.0)
        held = total.astype(BF16)
        arrived = [shift(held, right_two), shift(held, left_two)]
        if right_four_grad:
            arrived.append(shift(held, right_four_grad))
            arrived.append(shift(held, left_four_grad))
        group, other = local_kernel(sum_kernel, [piece, piece], moved=2 * small)(
            flags, held, *arrived
        )
        g = core(other)
        weight_grad = local_kernel(
            join_kernel,
            jax.ShapeDtypeStruct((quarter, features), BF16),
            moved=4 * quarter * features,
        )(flags, group, g)
        return output[None], hidden_grad[None], weight_grad[None]

    return compute


def solution(mesh):
    spec = P("ep", "dp", None)
    return jax.shard_map(
        make_body(mesh.shape["ep"], mesh.shape["dp"]),
        mesh=mesh,
        in_specs=(spec, spec, spec, P(), P("ep", "dp")),
        out_specs=(spec, spec, spec),
        check_vma=False,
    )
```

time: 129 us -> 110 us (0.85)
  the two profiles are of different devices: /device:TPU:0 before, /device:TPU:13 now
where the time goes in v3:
time: 110 us
  waiting for transfers between devices  50.4 us (46%)
  starting transfers between devices  35.5 us (32%)
  Pallas kernels  16.3 us (15%)
  local copies, waits for them, and re-layouts  5.12 us (5%)
  between operations  1.6 us (1%)
    ppermute x21, waiting for transfers between devices, permute(): return lax.ppermute(x, axes, pairs) if pairs else jnp.zeros_like(x)  50.4 us
    ppermute x21, starting transfers between devices, permute(): return lax.ppermute(x, axes, pairs) if pairs else jnp.zeros_like(x)  35.5 us
    pallas_call x10, Pallas kernels, call(): pl.pallas_call(kernel, out_shape=out_shapes, in_specs=[pl.BlockSpec(memor...  16.3 us
    unnamed x24, local copies, waits for them, and re-layouts  3.99 us
  transfers between devices with their start and end apart: 21, of which 11 were waited for; matrix products, arithmetic and copies ran while one was open for 1% of the time, Pallas kernels for 13%

profile of v3, /device:TPU:13, one launch (start us, length us, event | category | flops | bytes accessed | tf_op | source)
XLA Modules:
  0.0 110.0 jit_solution(15438086169495439558)
XLA Ops:
  0.7 0.0 copy-start.3
  0.7 1.1 dynamic-slice_bitcast_fusion
  1.7 0.0 copy-start
  1.8 0.7 collective-permute-start.6
  3.2 0.1 fusion.3
  3.3 0.1 fusion.6
  3.4 0.1 stack.78
  3.4 0.1 select_reduce_fusion.flags
  3.5 0.0 copy-start.1
  3.6 1.2 %copy-done.1 = bf16[1,256,2048]{2,1,0:T(8,128)(2,1)S(1)} copy-done((bf16[1,256,2048]{2,1,0:T(8,128)(2,1)S(1)}, bf16[1,256,2048]{2,1,0:T(8,128)(2,1)}, u32[]{:S(2)}) %copy-start.1) | copy-done | bytes 1048600
  4.8 0.7 shard_map.76
  5.4 0.7 collective-permute-start.4
  6.2 0.7 collective-permute-start.2
  6.9 0.6 shard_map.79
  7.5 3.1 %collective-permute-start.7 = (bf16[192,1024]{1,0:T(8,128)(2,1)S(1)}, bf16[192,1024]{1,0:T(8,128)(2,1)S(1)}, u32[]{:S(2)}, u32[]{:S(2)}) collective-permute-start(bf16[192,1024]{1,0:T(8,128)(2,1)S(1)} %shard_map.79), channel_id=1, source_target_pairs={{0,8},{4,12},{8,16},{12,20},{16,24},{20,28},{1,9},{5,13},{9,17},{1... | collective-permute-start | bytes 1179656 | tf_op jit(solution)/shard_map/ppermute | solution.py:249
  10.6 1.6 %collective-permute-start = (bf16[256,768]{1,0:T(8,128)(2,1)S(1)}, bf16[256,768]{1,0:T(8,128)(2,1)S(1)}, u32[]{:S(2)}, u32[]{:S(2)}) collective-permute-start(bf16[256,768]{1,0:T(8,128)(2,1)S(1)} %get-tuple-element.29.no), channel_id=1, source_target_pairs={{0,4},{4,0},{8,12},{12,8},{16,20},{20,16},{24,28},{28,24},{1,5},{5... | collective-permute-start | bytes 1179656 | tf_op jit(solution)/shard_map/ppermute | solution.py:249
  12.2 0.1 collective-permute-start.1
  12.3 0.0 collective-permute-done.4.yes
  12.3 0.6 shard_map.78
  12.9 7.5 %collective-permute-start.5 = (bf16[256,1024]{1,0:T(8,128)(2,1)S(1)}, bf16[256,1024]{1,0:T(8,128)(2,1)}, u32[]{:S(2)}, u32[]{:S(2)}) collective-permute-start(bf16[256,1024]{1,0:T(8,128)(2,1)S(1)} %shard_map.78), channel_id=1, source_target_pairs={{24,16},{4,12},{8,4},{20,24},{25,17},{5,13},{9,5},{21,25},{26,18},... | collective-permute-start | bytes 1572872 | tf_op jit(solution)/shard_map/ppermute | solution.py:249
  20.4 0.0 collective-permute-done.2.yes
  20.4 1.3 %shard_map.77 = bf16[256,768]{1,0:T(8,128)(2,1)} custom-call(s32[13]{0:T(128)S(1)} %select_reduce_fusion.flags, bf16[256,768]{1,0:T(8,128)(2,1)S(1)} %collective-permute-done.2.yes, bf16[256,768]{1,0:T(8,128)(2,1)S(1)} %get-tuple-element.29.no), custom_call_target="tpu_custom_call" | custom-call | bytes 786432 | tf_op jit(solution)/shard_map/pallas_call | solution.py:21
  21.8 3.7 %collective-permute-start.3 = (bf16[256,768]{1,0:T(8,128)(2,1)}, bf16[256,768]{1,0:T(8,128)(2,1)}, u32[]{:S(2)}, u32[]{:S(2)}) collective-permute-start(bf16[256,768]{1,0:T(8,128)(2,1)} %shard_map.77), channel_id=1, source_target_pairs={{24,16},{4,12},{8,4},{20,24},{25,17},{5,13},{9,5},{21,25},{26,18},... | collective-permute-start | bytes 1179656 | tf_op jit(solution)/shard_map/ppermute | solution.py:249
  25.5 0.0 collective-permute-done.7.came
  25.5 1.3 %shard_map.80.u = bf16[192,1024]{1,0:T(8,128)(2,1)} custom-call(s32[13]{0:T(128)S(1)} %select_reduce_fusion.flags, bf16[192,2048]{1,0:T(8,128)(2,1)S(1)} %bitcast.27, bf16[192,1024]{1,0:T(8,128)(2,1)S(1)} %collective-permute-done.6.partner_part, bf16[192,1024]{1,0:T(8,128)(2,1)S(1)} %collective-permute-done.7.came), custom_call_target="tpu_custom_call" | custom-call | bytes 1179648 | tf_op jit(solution)/shard_map/pallas_call | solution.py:21
  26.8 0.2 collective-permute-start.11
  27.0 0.7 copy-done.6
  27.7 2.4 %collective-permute-start.8 = (bf16[192,1024]{1,0:T(8,128)(2,1)}, bf16[192,1024]{1,0:T(8,128)(2,1)S(1)}, u32[]{:S(2)}, u32[]{:S(2)}) collective-permute-start(bf16[192,1024]{1,0:T(8,128)(2,1)} %shard_map.80.u), channel_id=1, source_target_pairs={{0,4},{1,2},{2,1},{3,7},{4,0},{5,6},{6,5},{7,3},{8,12},{9,10},{10,... | collective-permute-start | bytes 1179656 | tf_op jit(solution)/shard_map/ppermute | solution.py:249
  30.2 0.0 copy-start.4
  30.2 1.0 copy-done.4
  31.2 1.0 copy-done.7
  32.2 3.0 %shard_map.81 = (bf16[192,1024]{1,0:T(8,128)(2,1)S(1)}, bf16[192,1024]{1,0:T(8,128)(2,1)S(1)}, bf16[192,1024]{1,0:T(8,128)(2,1)S(1)}, bf16[192,1024]{1,0:T(8,128)(2,1)S(1)}) custom-call(s32[13]{0:T(128)S(1)} %select_reduce_fusion.flags, bf16[256,768]{1,0:T(8,128)(2,1)S(1)} %bitcast.32, bf16[256,2048]{1,0:T(8,128)(2,1)S(1)} %bitcast.29, ...), custom_call_target="tpu_custom_call" | custom-call | flops 1207959552 | bytes 4325376 | tf_op jit(solution)/shard_map/pallas_call | solution.py:21
  35.2 1.6 %collective-permute-done.11.a1 = bf16[192,1024]{1,0:T(8,128)(2,1)S(1)} collective-permute-done((bf16[192,1024]{1,0:T(8,128)(2,1)}, bf16[192,1024]{1,0:T(8,128)(2,1)S(1)}, u32[]{:S(2)}, u32[]{:S(2)}) %collective-permute-start.11) | collective-permute-done | bytes 393248 | tf_op jit(solution)/shard_map/ppermute | solution.py:249
  36.8 1.3 %collective-permute-start.12 = (bf16[192,1024]{1,0:T(8,128)(2,1)S(1)}, bf16[192,1024]{1,0:T(8,128)(2,1)S(1)}, u32[]{:S(2)}, u32[]{:S(2)}) collective-permute-start(bf16[192,1024]{1,0:T(8,128)(2,1)S(1)} %collective-permute-done.11.a1), channel_id=1, source_target_pairs={{0,4},{1,2},{2,1},{3,7},{4,0},{5,6},{6,5},{7,3},{8,12},{9,10},{10,... | collective-permute-start | bytes 1179656 | tf_op jit(solution)/shard_map/ppermute | solution.py:249
  38.1 0.3 collective-permute-done.8.m1
  38.4 0.1 broadcast_select_fusion.1
  38.4 0.1 collective-permute-start.9
  38.5 9.1 %collective-permute-done.12.m2 = bf16[192,1024]{1,0:T(8,128)(2,1)S(1)} collective-permute-done((bf16[192,1024]{1,0:T(8,128)(2,1)S(1)}, bf16[192,1024]{1,0:T(8,128)(2,1)S(1)}, u32[]{:S(2)}, u32[]{:S(2)}) %collective-permute-start.12) | collective-permute-done | bytes 393248 | tf_op jit(solution)/shard_map/ppermute | solution.py:249
  47.6 0.1 broadcast_select_fusion
  47.7 0.1 collective-permute-start.13
  47.8 1.6 %collective-permute-done.9.a2 = bf16[192,1024]{1,0:T(8,128)(2,1)S(1)} collective-permute-done((bf16[192,1024]{1,0:T(8,128)(2,1)S(1)}, bf16[192,1024]{1,0:T(8,128)(2,1)S(1)}, u32[]{:S(2)}, u32[]{:S(2)}) %collective-permute-start.9) | collective-permute-done | bytes 393248 | tf_op jit(solution)/shard_map/ppermute | solution.py:249
  49.3 0.1 add_convert_fusion.3
  49.5 2.0 %collective-permute-start.10 = (bf16[192,1024]{1,0:T(8,128)(2,1)S(1)}, bf16[192,1024]{1,0:T(8,128)(2,1)S(1)}, u32[]{:S(2)}, u32[]{:S(2)}) collective-permute-start(bf16[192,1024]{1,0:T(8,128)(2,1)S(1)} %add_convert_fusion.3), channel_id=1, source_target_pairs={{0,4},{1,2},{2,1},{3,7},{4,0},{5,6},{6,5},{7,3},{8,12},{9,10},{10,... | collective-permute-start | bytes 1179656 | tf_op jit(solution)/shard_map/ppermute | solution.py:249
  51.5 6.2 %collective-permute-done.13.a3 = bf16[192,1024]{1,0:T(8,128)(2,1)S(1)} collective-permute-done((bf16[192,1024]{1,0:T(8,128)(2,1)S(1)}, bf16[192,1024]{1,0:T(8,128)(2,1)S(1)}, u32[]{:S(2)}, u32[]{:S(2)}) %collective-permute-start.13) | collective-permute-done | bytes 393248 | tf_op jit(solution)/shard_map/ppermute | solution.py:249
  57.7 0.1 add_convert_fusion.1
  57.9 2.7 %collective-permute-done.10 = bf16[192,1024]{1,0:T(8,128)(2,1)S(1)} collective-permute-done((bf16[192,1024]{1,0:T(8,128)(2,1)S(1)}, bf16[192,1024]{1,0:T(8,128)(2,1)S(1)}, u32[]{:S(2)}, u32[]{:S(2)}) %collective-permute-start.10) | collective-permute-done | bytes 393248 | tf_op jit(solution)/shard_map/ppermute | solution.py:249
  60.5 0.1 fusion
  60.7 0.1 collective-permute-start.14
  60.8 1.2 %collective-permute-start.15 = (bf16[192,1024]{1,0:T(8,128)(2,1)S(1)}, bf16[192,1024]{1,0:T(8,128)(2,1)S(1)}, u32[]{:S(2)}, u32[]{:S(2)}) collective-permute-start(bf16[192,1024]{1,0:T(8,128)(2,1)S(1)} %add_convert_fusion.1), channel_id=1, source_target_pairs={{0,4},{1,2},{2,1},{3,7},{4,0},{5,6},{6,5},{7,3},{8,12},{9,10},{10,... | collective-permute-start | bytes 1179656 | tf_op jit(solution)/shard_map/ppermute | solution.py:249
  62.0 4.8 %shard_map.82 = (bf16[256,1024]{1,0:T(8,128)(2,1)S(1)}, f32[256,768]{1,0:T(8,128)S(1)}, bf16[256,1792]{1,0:T(8,128)(2,1)S(1)}, bf16[256,1792]{1,0:T(8,128)(2,1)S(1)}) custom-call(s32[13]{0:T(128)S(1)} %select_reduce_fusion.flags, bf16[256,768]{1,0:T(8,128)(2,1)S(1)} %bitcast.33, bf16[256,2048]{1,0:T(8,128)(2,1)S(1)} %bitcast.30, ...), custom_call_target="tpu_custom_call" | custom-call | flops 2415919104 | bytes 7077888 | tf_op jit(solution)/shard_map/pallas_call | solution.py:21
  66.8 3.6 %collective-permute-done.14 = bf16[192,1024]{1,0:T(8,128)(2,1)S(1)} collective-permute-done((bf16[192,1024]{1,0:T(8,128)(2,1)S(1)}, bf16[192,1024]{1,0:T(8,128)(2,1)S(1)}, u32[]{:S(2)}, u32[]{:S(2)}) %collective-permute-start.14) | collective-permute-done | bytes 393248 | tf_op jit(solution)/shard_map/ppermute | solution.py:249
  70.4 0.1 collective-permute-done.15
  70.5 1.9 %collective-permute-start.16 = (bf16[256,1792]{1,0:T(8,128)(2,1)S(1)}, bf16[256,1792]{1,0:T(8,128)(2,1)S(1)}, u32[]{:S(2)}, u32[]{:S(2)}) collective-permute-start(bf16[256,1792]{1,0:T(8,128)(2,1)S(1)} %get-tuple-element.42), channel_id=1, source_target_pairs={{0,4},{4,0},{8,12},{12,8},{16,20},{20,16},{24,28},{28,24},{1,5},{5... | collective-permute-start | bytes 2752520 | tf_op jit(solution)/shard_map/ppermute | solution.py:249
  72.4 1.3 %collective-permute-start.17 = (bf16[256,1792]{1,0:T(8,128)(2,1)S(1)}, bf16[256,1792]{1,0:T(8,128)(2,1)S(1)}, u32[]{:S(2)}, u32[]{:S(2)}) collective-permute-start(bf16[256,1792]{1,0:T(8,128)(2,1)S(1)} %get-tuple-element.43), channel_id=1, source_target_pairs={{4,8},{16,12},{12,16},{24,20},{5,9},{17,13},{13,17},{25,21},{6,10}... | collective-permute-start | bytes 2752520 | tf_op jit(solution)/shard_map/ppermute | solution.py:249
  73.7 0.2 add_convert_fusion.held
  73.9 4.8 %collective-permute-start.19 = (bf16[192,1024]{1,0:T(8,128)(2,1)S(1)}, bf16[192,1024]{1,0:T(8,128)(2,1)S(1)}, u32[]{:S(2)}, u32[]{:S(2)}) collective-permute-start(bf16[192,1024]{1,0:T(8,128)(2,1)S(1)} %add_convert_fusion.held), channel_id=1, source_target_pairs={{8,0},{12,4},{16,8},{20,12},{24,16},{28,20},{9,1},{13,5},{17,9},{2... | collective-permute-start | bytes 1179656 | tf_op jit(solution)/shard_map/ppermute | solution.py:249
  78.7 1.9 %collective-permute-start.18 = (bf16[192,1024]{1,0:T(8,128)(2,1)S(1)}, bf16[192,1024]{1,0:T(8,128)(2,1)S(1)}, u32[]{:S(2)}, u32[]{:S(2)}) collective-permute-start(bf16[192,1024]{1,0:T(8,128)(2,1)S(1)} %add_convert_fusion.held), channel_id=1, source_target_pairs={{0,8},{4,12},{8,16},{12,20},{16,24},{20,28},{1,9},{5,13},{9,17},{1... | collective-permute-start | bytes 1179656 | tf_op jit(solution)/shard_map/ppermute | solution.py:249
  80.6 7.0 %collective-permute-done.19.right = bf16[192,1024]{1,0:T(8,128)(2,1)S(1)} collective-permute-done((bf16[192,1024]{1,0:T(8,128)(2,1)S(1)}, bf16[192,1024]{1,0:T(8,128)(2,1)S(1)}, u32[]{:S(2)}, u32[]{:S(2)}) %collective-permute-start.19) | collective-permute-done | bytes 393248 | tf_op jit(solution)/shard_map/ppermute | solution.py:249
  87.6 16.6 %collective-permute-done.18.left = bf16[192,1024]{1,0:T(8,128)(2,1)S(1)} collective-permute-done((bf16[192,1024]{1,0:T(8,128)(2,1)S(1)}, bf16[192,1024]{1,0:T(8,128)(2,1)S(1)}, u32[]{:S(2)}, u32[]{:S(2)}) %collective-permute-start.18) | collective-permute-done | bytes 393248 | tf_op jit(solution)/shard_map/ppermute | solution.py:249
  104.1 0.8 shard_map.84
  104.9 0.1 collective-permute-start.20
  105.0 1.7 %collective-permute-done.20.other = bf16[192,1024]{1,0:T(8,128)(2,1)S(1)} collective-permute-done((bf16[192,1024]{1,0:T(8,128)(2,1)S(1)}, bf16[192,1024]{1,0:T(8,128)(2,1)S(1)}, u32[]{:S(2)}, u32[]{:S(2)}) %collective-permute-start.20) | collective-permute-done | bytes 393248 | tf_op jit(solution)/shard_map/ppermute | solution.py:249
  106.7 1.5 %shard_map.85 = bf16[192,2048]{1,0:T(8,128)(2,1)} custom-call(s32[13]{0:T(128)S(1)} %select_reduce_fusion.flags, bf16[192,1024]{1,0:T(8,128)(2,1)S(1)} %get-tuple-element.49.own, bf16[192,1024]{1,0:T(8,128)(2,1)S(1)} %collective-permute-done.20.other), custom_call_target="tpu_custom_call" | custom-call | bytes 1572864 | tf_op jit(solution)/shard_map/pallas_call | solution.py:21
  108.2 1.8 %shard_map.83 = (bf16[256,2048]{1,0:T(8,128)(2,1)}, bf16[256,768]{1,0:T(8,128)(2,1)}) custom-call(s32[13]{0:T(128)S(1)} %select_reduce_fusion.flags, bf16[256,1024]{1,0:T(8,128)(2,1)S(1)} %get-tuple-element.36.out, f32[256,768]{1,0:T(8,128)S(1)} %get-tuple-element.37.hg, bf16[256,1792]{1,0:T(8,128)(2,1)S(1)} %collective-permute-done.16.core, ...), custom_call_target="tpu_custom_call" | custom-call | bytes 3670016 | tf_op jit(solution)/shard_map/pallas_call | solution.py:21
  (28 shorter events, 0.1 us)
Async XLA Ops:
  0.6 2.5 %copy-start.11 = (s32[8]{0:T(128)S(1)}, s32[8]{0:T(128)}, u32[]{:S(2)}) copy-start(s32[8]{0:T(128)} %param.8) | copy-start | bytes 100
  0.7 2.9 %copy-start.3 = (bf16[1,256,768]{2,1,0:T(8,128)(2,1)S(1)}, bf16[1,256,768]{2,1,0:T(8,128)(2,1)}, u32[]{:S(2)}) copy-start(bf16[1,256,768]{2,1,0:T(8,128)(2,1)} %param.5) | copy-start | bytes 1179652
  1.7 5.1 %copy-start = (bf16[1,192,2048]{2,1,0:T(8,128)(2,1)S(1)}, bf16[1,192,2048]{2,1,0:T(8,128)(2,1)}, u32[]{:S(2)}) copy-start(bf16[1,192,2048]{2,1,0:T(8,128)(2,1)} %param.7) | copy-start | bytes 2359300
  1.8 5.1 %collective-permute-start.6 = (bf16[192,1024]{1,0:T(8,128)(2,1)S(1)}, bf16[192,1024]{1,0:T(8,128)(2,1)S(1)}, u32[]{:S(2)}, u32[]{:S(2)}) collective-permute-start(bf16[192,1024]{1,0:T(8,128)(2,1)S(1)} %dynamic-slice_bitcast_fusion), channel_id=1, source_target_pairs={{0,4},{4,0},{8,12},{12,8},{16,20},{20,16},{24,28},{28,24},{1,5},{5... | collective-permute-start | bytes 1179656 | tf_op jit(solution)/shard_map/ppermute | solution.py:249
  3.5 1.2 %copy-start.1 = (bf16[1,256,2048]{2,1,0:T(8,128)(2,1)S(1)}, bf16[1,256,2048]{2,1,0:T(8,128)(2,1)}, u32[]{:S(2)}) copy-start(bf16[1,256,2048]{2,1,0:T(8,128)(2,1)} %param.6) | copy-start | bytes 3145732
  5.4 6.9 %collective-permute-start.4 = (bf16[256,1024]{1,0:T(8,128)(2,1)S(1)}, bf16[256,1024]{1,0:T(8,128)(2,1)S(1)}, u32[]{:S(2)}, u32[]{:S(2)}) collective-permute-start(bf16[256,1024]{1,0:T(8,128)(2,1)S(1)} %get-tuple-element.30.no), channel_id=1, source_target_pairs={{12,24},{16,4},{13,25},{17,5},{14,26},{18,6},{15,27},{19,7}} | collective-permute-start | bytes 1572872 | tf_op jit(solution)/shard_map/ppermute | solution.py:249
  6.2 14.3 %collective-permute-start.2 = (bf16[256,768]{1,0:T(8,128)(2,1)S(1)}, bf16[256,768]{1,0:T(8,128)(2,1)S(1)}, u32[]{:S(2)}, u32[]{:S(2)}) collective-permute-start(bf16[256,768]{1,0:T(8,128)(2,1)S(1)} %get-tuple-element.29.no), channel_id=1, source_target_pairs={{12,24},{16,4},{13,25},{17,5},{14,26},{18,6},{15,27},{19,7}} | collective-permute-start | bytes 1179656 | tf_op jit(solution)/shard_map/ppermute | solution.py:249
  7.5 18.0 %collective-permute-start.7 = (bf16[192,1024]{1,0:T(8,128)(2,1)S(1)}, bf16[192,1024]{1,0:T(8,128)(2,1)S(1)}, u32[]{:S(2)}, u32[]{:S(2)}) collective-permute-start(bf16[192,1024]{1,0:T(8,128)(2,1)S(1)} %shard_map.79), channel_id=1, source_target_pairs={{0,8},{4,12},{8,16},{12,20},{16,24},{20,28},{1,9},{5,13},{9,17},{1... | collective-permute-start | bytes 1179656 | tf_op jit(solution)/shard_map/ppermute | solution.py:249
  10.6 16.4 %collective-permute-start = (bf16[256,768]{1,0:T(8,128)(2,1)S(1)}, bf16[256,768]{1,0:T(8,128)(2,1)S(1)}, u32[]{:S(2)}, u32[]{:S(2)}) collective-permute-start(bf16[256,768]{1,0:T(8,128)(2,1)S(1)} %get-tuple-element.29.no), channel_id=1, source_target_pairs={{0,4},{4,0},{8,12},{12,8},{16,20},{20,16},{24,28},{28,24},{1,5},{5... | collective-permute-start | bytes 1179656 | tf_op jit(solution)/shard_map/ppermute | solution.py:249
  12.2 17.9 %collective-permute-start.1 = (bf16[256,1024]{1,0:T(8,128)(2,1)S(1)}, bf16[256,1024]{1,0:T(8,128)(2,1)}, u32[]{:S(2)}, u32[]{:S(2)}) collective-permute-start(bf16[256,1024]{1,0:T(8,128)(2,1)S(1)} %get-tuple-element.30.no), channel_id=1, source_target_pairs={{0,4},{4,0},{8,12},{12,8},{16,20},{20,16},{24,28},{28,24},{1,5},{5... | collective-permute-start | bytes 1572872 | tf_op jit(solution)/shard_map/ppermute | solution.py:249
  12.9 17.3 %collective-permute-start.5 = (bf16[256,1024]{1,0:T(8,128)(2,1)S(1)}, bf16[256,1024]{1,0:T(8,128)(2,1)}, u32[]{:S(2)}, u32[]{:S(2)}) collective-permute-start(bf16[256,1024]{1,0:T(8,128)(2,1)S(1)} %shard_map.78), channel_id=1, source_target_pairs={{24,16},{4,12},{8,4},{20,24},{25,17},{5,13},{9,5},{21,25},{26,18},... | collective-permute-start | bytes 1572872 | tf_op jit(solution)/shard_map/ppermute | solution.py:249
  21.8 8.4 %copy-start.2 = (bf16[1,256,2048]{2,1,0:T(8,128)(2,1)S(1)}, bf16[1,256,2048]{2,1,0:T(8,128)(2,1)}, u32[]{:S(2)}) copy-start(bf16[1,256,2048]{2,1,0:T(8,128)(2,1)} %param.6) | copy-start | bytes 3145732
  21.8 8.4 %collective-permute-start.3 = (bf16[256,768]{1,0:T(8,128)(2,1)}, bf16[256,768]{1,0:T(8,128)(2,1)}, u32[]{:S(2)}, u32[]{:S(2)}) collective-permute-start(bf16[256,768]{1,0:T(8,128)(2,1)} %shard_map.77), channel_id=1, source_target_pairs={{24,16},{4,12},{8,4},{20,24},{25,17},{5,13},{9,5},{21,25},{26,18},... | collective-permute-start | bytes 1179656 | tf_op jit(solution)/shard_map/ppermute | solution.py:249
  26.8 10.0 %collective-permute-start.11 = (bf16[192,1024]{1,0:T(8,128)(2,1)}, bf16[192,1024]{1,0:T(8,128)(2,1)S(1)}, u32[]{:S(2)}, u32[]{:S(2)}) collective-permute-start(bf16[192,1024]{1,0:T(8,128)(2,1)} %shard_map.80.u), channel_id=1, source_target_pairs={{0,1},{1,0},{2,3},{3,2},{4,5},{5,4},{6,7},{7,6},{8,9},{9,8},{10,11... | collective-permute-start | bytes 1179656 | tf_op jit(solution)/shard_map/ppermute | solution.py:249
  27.0 0.7 copy-start.6
  27.7 10.7 %collective-permute-start.8 = (bf16[192,1024]{1,0:T(8,128)(2,1)}, bf16[192,1024]{1,0:T(8,128)(2,1)S(1)}, u32[]{:S(2)}, u32[]{:S(2)}) collective-permute-start(bf16[192,1024]{1,0:T(8,128)(2,1)} %shard_map.80.u), channel_id=1, source_target_pairs={{0,4},{1,2},{2,1},{3,7},{4,0},{5,6},{6,5},{7,3},{8,12},{9,10},{10,... | collective-permute-start | bytes 1179656 | tf_op jit(solution)/shard_map/ppermute | solution.py:249
  30.2 1.0 copy-start.4
  31.2 1.0 copy-start.7
  36.8 1.6 %copy-start.9 = (bf16[192,1024]{1,0:T(8,128)(2,1)}, bf16[192,1024]{1,0:T(8,128)(2,1)S(1)}, u32[]{:S(2)}) copy-start(bf16[192,1024]{1,0:T(8,128)(2,1)S(1)} %collective-permute-done.11.a1) | copy-start | bytes 1179652
  36.8 10.8 %collective-permute-start.12 = (bf16[192,1024]{1,0:T(8,128)(2,1)S(1)}, bf16[192,1024]{1,0:T(8,128)(2,1)S(1)}, u32[]{:S(2)}, u32[]{:S(2)}) collective-permute-start(bf16[192,1024]{1,0:T(8,128)(2,1)S(1)} %collective-permute-done.11.a1), channel_id=1, source_target_pairs={{0,4},{1,2},{2,1},{3,7},{4,0},{5,6},{6,5},{7,3},{8,12},{9,10},{10,... | collective-permute-start | bytes 1179656 | tf_op jit(solution)/shard_map/ppermute | solution.py:249
  38.4 10.9 %collective-permute-start.9 = (bf16[192,1024]{1,0:T(8,128)(2,1)S(1)}, bf16[192,1024]{1,0:T(8,128)(2,1)S(1)}, u32[]{:S(2)}, u32[]{:S(2)}) collective-permute-start(bf16[192,1024]{1,0:T(8,128)(2,1)S(1)} %broadcast_select_fusion.1), channel_id=1, source_target_pairs={{0,1},{1,0},{2,3},{3,2},{4,5},{5,4},{6,7},{7,6},{8,9},{9,8},{10,11... | collective-permute-start | bytes 1179656 | tf_op jit(solution)/shard_map/ppermute | solution.py:249
  47.7 10.0 %collective-permute-start.13 = (bf16[192,1024]{1,0:T(8,128)(2,1)S(1)}, bf16[192,1024]{1,0:T(8,128)(2,1)S(1)}, u32[]{:S(2)}, u32[]{:S(2)}) collective-permute-start(bf16[192,1024]{1,0:T(8,128)(2,1)S(1)} %broadcast_select_fusion), channel_id=1, source_target_pairs={{0,1},{1,0},{2,3},{3,2},{4,5},{5,4},{6,7},{7,6},{8,9},{9,8},{10,11... | collective-permute-start | bytes 1179656 | tf_op jit(solution)/shard_map/ppermute | solution.py:249
  49.5 11.1 %collective-permute-start.10 = (bf16[192,1024]{1,0:T(8,128)(2,1)S(1)}, bf16[192,1024]{1,0:T(8,128)(2,1)S(1)}, u32[]{:S(2)}, u32[]{:S(2)}) collective-permute-start(bf16[192,1024]{1,0:T(8,128)(2,1)S(1)} %add_convert_fusion.3), channel_id=1, source_target_pairs={{0,4},{1,2},{2,1},{3,7},{4,0},{5,6},{6,5},{7,3},{8,12},{9,10},{10,... | collective-permute-start | bytes 1179656 | tf_op jit(solution)/shard_map/ppermute | solution.py:249
  60.5 1.5 %copy-start.5 = (bf16[1,256,768]{2,1,0:T(8,128)(2,1)S(1)}, bf16[1,256,768]{2,1,0:T(8,128)(2,1)}, u32[]{:S(2)}) copy-start(bf16[1,256,768]{2,1,0:T(8,128)(2,1)} %param.5) | copy-start | bytes 1179652
  60.5 1.5 %copy-start.8 = (bf16[256,768]{1,0:T(8,128)(2,1)S(1)}, bf16[256,768]{1,0:T(8,128)(2,1)}, u32[]{:S(2)}) copy-start(bf16[256,768]{1,0:T(8,128)(2,1)} %copy-done.6) | copy-start | bytes 1179652
  60.5 1.5 %copy-start.10 = (bf16[192,1024]{1,0:T(8,128)(2,1)S(1)}, bf16[192,1024]{1,0:T(8,128)(2,1)}, u32[]{:S(2)}) copy-start(bf16[192,1024]{1,0:T(8,128)(2,1)} %copy-done.9) | copy-start | bytes 1179652
  60.7 9.7 %collective-permute-start.14 = (bf16[192,1024]{1,0:T(8,128)(2,1)S(1)}, bf16[192,1024]{1,0:T(8,128)(2,1)S(1)}, u32[]{:S(2)}, u32[]{:S(2)}) collective-permute-start(bf16[192,1024]{1,0:T(8,128)(2,1)S(1)} %fusion), channel_id=1, source_target_pairs={{0,1},{1,0},{2,3},{3,2},{4,5},{5,4},{6,7},{7,6},{8,9},{9,8},{10,11... | collective-permute-start | bytes 1179656 | tf_op jit(solution)/shard_map/ppermute | solution.py:249
  60.8 9.7 %collective-permute-start.15 = (bf16[192,1024]{1,0:T(8,128)(2,1)S(1)}, bf16[192,1024]{1,0:T(8,128)(2,1)S(1)}, u32[]{:S(2)}, u32[]{:S(2)}) collective-permute-start(bf16[192,1024]{1,0:T(8,128)(2,1)S(1)} %add_convert_fusion.1), channel_id=1, source_target_pairs={{0,4},{1,2},{2,1},{3,7},{4,0},{5,6},{6,5},{7,3},{8,12},{9,10},{10,... | collective-permute-start | bytes 1179656 | tf_op jit(solution)/shard_map/ppermute | solution.py:249
  70.5 37.7 %collective-permute-start.16 = (bf16[256,1792]{1,0:T(8,128)(2,1)S(1)}, bf16[256,1792]{1,0:T(8,128)(2,1)S(1)}, u32[]{:S(2)}, u32[]{:S(2)}) collective-permute-start(bf16[256,1792]{1,0:T(8,128)(2,1)S(1)} %get-tuple-element.42), channel_id=1, source_target_pairs={{0,4},{4,0},{8,12},{12,8},{16,20},{20,16},{24,28},{28,24},{1,5},{5... | collective-permute-start | bytes 2752520 | tf_op jit(solution)/shard_map/ppermute | solution.py:249
  72.4 35.8 %collective-permute-start.17 = (bf16[256,1792]{1,0:T(8,128)(2,1)S(1)}, bf16[256,1792]{1,0:T(8,128)(2,1)S(1)}, u32[]{:S(2)}, u32[]{:S(2)}) collective-permute-start(bf16[256,1792]{1,0:T(8,128)(2,1)S(1)} %get-tuple-element.43), channel_id=1, source_target_pairs={{4,8},{16,12},{12,16},{24,20},{5,9},{17,13},{13,17},{25,21},{6,10}... | collective-permute-start | bytes 2752520 | tf_op jit(solution)/shard_map/ppermute | solution.py:249
  73.9 13.7 %collective-permute-start.19 = (bf16[192,1024]{1,0:T(8,128)(2,1)S(1)}, bf16[192,1024]{1,0:T(8,128)(2,1)S(1)}, u32[]{:S(2)}, u32[]{:S(2)}) collective-permute-start(bf16[192,1024]{1,0:T(8,128)(2,1)S(1)} %add_convert_fusion.held), channel_id=1, source_target_pairs={{8,0},{12,4},{16,8},{20,12},{24,16},{28,20},{9,1},{13,5},{17,9},{2... | collective-permute-start | bytes 1179656 | tf_op jit(solution)/shard_map/ppermute | solution.py:249
  78.7 25.5 %collective-permute-start.18 = (bf16[192,1024]{1,0:T(8,128)(2,1)S(1)}, bf16[192,1024]{1,0:T(8,128)(2,1)S(1)}, u32[]{:S(2)}, u32[]{:S(2)}) collective-permute-start(bf16[192,1024]{1,0:T(8,128)(2,1)S(1)} %add_convert_fusion.held), channel_id=1, source_target_pairs={{0,8},{4,12},{8,16},{12,20},{16,24},{20,28},{1,9},{5,13},{9,17},{1... | collective-permute-start | bytes 1179656 | tf_op jit(solution)/shard_map/ppermute | solution.py:249
  104.9 1.8 %collective-permute-start.20 = (bf16[192,1024]{1,0:T(8,128)(2,1)S(1)}, bf16[192,1024]{1,0:T(8,128)(2,1)S(1)}, u32[]{:S(2)}, u32[]{:S(2)}) collective-permute-start(bf16[192,1024]{1,0:T(8,128)(2,1)S(1)} %get-tuple-element.50), channel_id=1, source_target_pairs={{0,4},{4,0},{8,12},{12,8},{16,20},{20,16},{24,28},{28,24},{1,5},{5... | collective-permute-start | bytes 1179656 | tf_op jit(solution)/shard_map/ppermute | solution.py:249

commit v4 on v3

--- a/solution.py
+++ b/solution.py
@@ -11,17 +11,19 @@
 BLOCK = 128
 FLAGS = (
     "odd", "z", "count", "partner", "helps", "begins", "before_two",
-    "after_two", "export_own", "far_weight", "far_grad", "relay", "by_one",
+    "after_two", "export_own", "far_weight", "far_grad", "relay", "by_one", "place",
 )
 
 
-def local_kernel(kernel, out_shapes, scratch=(), flops=0, moved=0, mib=8):
+def local_kernel(kernel, out_shapes, scratch=(), flops=0, moved=0, mib=8, in_hbm=0):
     def call(flags, *arrays):
         vmem = pl.BlockSpec(memory_space=pltpu.VMEM)
         return pl.pallas_call(
             kernel,
             out_shape=out_shapes,
-            in_specs=[pl.BlockSpec(memory_space=pltpu.SMEM)] + [vmem] * len(arrays),
+            in_specs=[pl.BlockSpec(memory_space=pltpu.SMEM)]
+            + [vmem] * (len(arrays) - in_hbm)
+            + [pl.BlockSpec(memory_space=pltpu.HBM)] * in_hbm,
             out_specs=jax.tree.map(lambda _: vmem, out_shapes),
             scratch_shapes=list(scratch),
             compiler_params=pltpu.CompilerParams(vmem_limit_bytes=mib << 20),
@@ -50,13 +52,15 @@
     return jnp.where(keep, x, jnp.zeros_like(x))
 
 
-def pack_kernel(flags, hid, cot, sent_h, sent_c):
+def pack_kernel(flags, hid, cot, sent_h, sent_c, own_c):
     half = cot.shape[1] // 2
+    own = cols(flag(flags, "odd") * half, half)
     other = cols((1 - flag(flags, "odd")) * half, half)
 
     def store(r, live):
         sent_h[r, :] = masked(live, hid[r, :])
         sent_c[r, :] = masked(live, cot[r, other])
+        own_c[r, :] = masked(live, cot[r, own])
 
     copy_live(flags, hid.shape[0], store)
 
@@ -104,38 +108,50 @@
         out[...] = came[...]
 
 
-def grad_kernel(flags, hid, cot, core_h, core_c, near_h, near_c, t0, t1, t2, t3, ht, cs):
-    rows, units = hid.shape
-    half = cot.shape[1] // 2
-    own = cols(flag(flags, "odd") * half, half)
-
-    def store(r, live):
-        cs[r, :] = masked(live, cot[r, own])
-
-    copy_live(flags, rows, store)
+def grad_kernel(flags, own_h, own_c, core_h, core_c, from_h, from_c,
+                t0, t1, t2, t3, near_h, near_c, ht, cs, sems):
+    rows, units = own_h.shape
+    copies = [
+        pltpu.make_async_copy(from_h, near_h, sems.at[0]),
+        pltpu.make_async_copy(from_c, near_c, sems.at[1]),
+    ]
+    for copy in copies:
+        copy.start()
+    cs[:rows, :] = own_c[...]
     cs[rows : 2 * rows, :] = masked(flag(flags, "partner") != 0, core_c[...])
+    ht[:, :rows] = own_h[...].T
+    ht[:, rows : 2 * rows] = core_h[...].T
+    for copy in copies:
+        copy.wait()
+    ht[:, 2 * rows :] = near_h[...].T
     cs[2 * rows :, :] = masked(flag(flags, "helps") != 0, near_c[...])
-    ht[:, :rows] = hid[...].T
-    ht[:, rows : 2 * rows] = core_h[...].T
-    ht[:, 2 * rows :] = near_h[...].T
     z = flag(flags, "z")
     quarter = units // 4
-    for k, term in enumerate((t0, t1, t2, t3)):
+    for k, term in ((3, t3), (2, t2), (1, t1), (0, t0)):
         at = pl.multiple_of((z ^ k) * quarter, 16)
         term[...] = jnp.dot(
             ht[pl.ds(at, quarter), :], cs[...], preferred_element_type=F32
         ).astype(BF16)
 
 
-def sum_kernel(flags, held, left, right, *rest):
-    far, own, other = rest[:-2], rest[-2], rest[-1]
+def sum_kernel(flags, held, beside, crossed, relayed, *rest):
+    outer, own, other = rest[:-2], rest[-2], rest[-1]
     none = jnp.zeros((), F32)
-
-    def add(x, keep):
-        return jnp.where(keep, x[...].astype(F32), none)
-
-    total = held[...].astype(F32) + add(left, flag(flags, "before_two") != 0)
-    own[...] = (total + add(right, flag(flags, "after_two") != 0)).astype(BF16)
+    place = flag(flags, "place")
+
+    def pick(direct, passed, outside, ref):
+        got = beside[...].astype(F32)
+        got = jnp.where(place == direct, crossed[...].astype(F32), got)
+        got = jnp.where(place == passed, relayed[...].astype(F32), got)
+        if outer:
+            got = jnp.where(place // 2 == outside, outer[ref][...].astype(F32), got)
+        return got
+
+    left, right = pick(4, 5, 0, 0), pick(3, 2, 3, 1)
+    total = held[...].astype(F32)
+    total = total + jnp.where(flag(flags, "before_two") != 0, left, none)
+    total = total + jnp.where(flag(flags, "after_two") != 0, right, none)
+    own[...] = total.astype(BF16)
 
     @pl.when(flag(flags, "partner") != 0)
     def _():
@@ -144,17 +160,17 @@
     @pl.when(flag(flags, "partner") == 0)
     def _():
         odd = flag(flags, "odd") != 0
-        theirs = jnp.where(odd, left[...].astype(F32), right[...].astype(F32))
-        if far:
-            more = jnp.where(odd, far[0][...].astype(F32), far[1][...].astype(F32))
+        theirs = jnp.where(odd, left, right)
+        if outer:
+            more = jnp.where(odd, outer[2][...].astype(F32), outer[3][...].astype(F32))
             theirs = theirs + jnp.where(flag(flags, "far_grad") != 0, more, none)
         other[...] = theirs.astype(BF16)
 
 
-def forward_kernel(flags, hid, cot, core_h, core_c, near_h, near_c, u, a1, m1, a2, m2, a3,
+def forward_kernel(flags, own_h, own_c, core_h, core_c, near_h, near_c, u, a1, m1, a2, m2, a3,
                    out, hg, to_core, to_near, weight):
-    rows, units = hid.shape
-    half = cot.shape[1] // 2
+    units = own_h.shape[1]
+    half = own_c.shape[1]
     z = flag(flags, "z")
     middle = (z == 1) | (z == 2)
     quarter = units // 4
@@ -176,7 +192,6 @@
         place(2, a2[...])
         place(3, a3[...])
 
-    own = cols(flag(flags, "odd") * half, half)
     w = weight[...]
 
     def products(h, c):
@@ -184,12 +199,9 @@
         g = lax.dot_general(c, w, (((1,), (1,)), ((), ())), preferred_element_type=F32)
         return o, g
 
-    def own_rows(r, live):
-        o, g = products(masked(live, hid[r, :]), masked(live, cot[r, own]))
-        out[r, :] = o.astype(BF16)
-        hg[r, :] = g
-
-    copy_live(flags, rows, own_rows)
+    o, g = products(own_h[...], own_c[...])
+    out[...] = o.astype(BF16)
+    hg[...] = g
     for h, c, dst in ((core_h, core_c, to_core), (near_h, near_c, to_near)):
         o, g = products(h[...], c[...])
         dst[:, :half] = o.astype(BF16)
@@ -222,7 +234,7 @@
 
 
 def make_body(n_ep, n_dp):
-    assert n_dp == 4 and n_ep % 2 == 0
+    assert n_dp == 4 and n_ep % 8 == 0
     both = ("ep", "dp")
     core_pairs = [(s, s ^ 1) for s in range(n_ep)]
     help_pairs = [(s, s + 1 if s % 2 else s - 1) for s in range(2, n_ep - 2)]
@@ -234,7 +246,12 @@
     hop_two = [(a ^ 5, b) for a, b in far] + [p for p in near if p[0] not in relays]
     by_one = {b for a, b in near if a in relays}
     right_two = [(s, s + 2) for s in range(n_ep - 2)]
-    left_two = [(s + 2, s) for s in range(n_ep - 2)]
+    beside_pairs = [(s, s ^ 2) for s in range(n_ep)]
+    moves = {2: 2, 5: -2, 3: 4, 4: -4}
+    crossing = [(s, s + moves[s % 8]) for s in range(n_ep) if s % 8 in moves]
+    relayed = [(s, s ^ 2) for s in range(n_ep) if s % 8 in (0, 7)]
+    block_right = [(s, s + 2) for s in range(n_ep - 2) if s % 8 > 5]
+    block_left = [(b, a) for a, b in block_right]
     right_four_weight = [(s - 4, s) for s in range(6, n_ep - 2, 2)]
     right_four_grad = [(s - 4, s) for s in range(7, n_ep - 2, 2)]
     left_four_grad = [(s + 4, s) for s in range(2, n_ep - 7, 2)]
@@ -291,6 +308,7 @@
             "far_grad": jnp.where(odd, e[-4] == e[-1], e[4] == e[1]),
             "relay": among(relays),
             "by_one": among(by_one),
+            "place": places % 8,
         }
         table = jnp.stack([rows[name].astype(jnp.int32) for name in FLAGS])
         return jnp.sum(jnp.where(places == s, table, 0), axis=1)
@@ -332,8 +350,8 @@
             flags, stored, partner_part, came
         )
 
-        sent_h, sent_c = local_kernel(
-            pack_kernel, [h_piece, c_piece], moved=4 * capacity * wide
+        sent_h, sent_c, own_c = local_kernel(
+            pack_kernel, [h_piece, c_piece, c_piece], moved=4 * capacity * wide
         )(flags, hid, cot)
 
         def to_neighbour(x):
@@ -348,17 +366,19 @@
 
         near = [to_neighbour(sent_h), to_neighbour(sent_c)]
         from_core = [core(sent_h), core(sent_c)]
-        terms = local_kernel(
+        *terms, near_h, near_c = local_kernel(
             grad_kernel,
-            [piece] * 4,
+            [piece] * 4 + [h_piece, c_piece],
             [
                 pltpu.VMEM((units, 3 * capacity), BF16),
                 pltpu.VMEM((3 * capacity, half), BF16),
+                pltpu.SemaphoreType.DMA((2,)),
             ],
             flops=6 * capacity * units * half,
             moved=2 * units * half + 6 * capacity * wide,
             mib=16,
-        )(flags, hid, cot, *from_core, *near)
+            in_hbm=2,
+        )(flags, sent_h, own_c, *from_core, *near)
 
         a1 = side(unit)
         m1 = middle(unit)
@@ -386,7 +406,7 @@
             flops=12 * capacity * units * half,
             moved=2 * units * half + 12 * capacity * wide,
             mib=24,
-        )(flags, hid, cot, *from_core, *near, unit, a1, m1, a2, m2, a3)
+        )(flags, sent_h, own_c, *from_core, near_h, near_c, unit, a1, m1, a2, m2, a3)
         a4, m4, to_core, to_next = lax.optimization_barrier((a4, m4, to_core, to_next))
         output, hidden_grad = local_kernel(
             output_kernel,
@@ -400,14 +420,20 @@
         total = a4.astype(F32) + terms[0].astype(F32)
         total = total + jnp.where(is_middle, m4.astype(F32), 0.0)
         held = total.astype(BF16)
-        arrived = [shift(held, right_two), shift(held, left_two)]
-        if right_four_grad:
-            arrived.append(shift(held, right_four_grad))
-            arrived.append(shift(held, left_four_grad))
+        crossed = shift(held, crossing)
+        arrived = [shift(held, beside_pairs), crossed, shift(crossed, relayed)]
+        if n_ep > 8:
+            arrived += [
+                shift(held, block_right),
+                shift(held, block_left),
+                shift(held, right_four_grad),
+                shift(held, left_four_grad),
+            ]
         group, other = local_kernel(sum_kernel, [piece, piece], moved=2 * small)(
             flags, held, *arrived
         )
         g = core(other)
+        g, output, hidden_grad = lax.optimization_barrier((g, output, hidden_grad))
         weight_grad = local_kernel(
             join_kernel,
             jax.ShapeDtypeStruct((quarter, features), BF16),

time: 110 us -> 110 us (level)
  waiting for transfers between devices: 50.4 us -> 37.5 us
  starting transfers between devices: 35.5 us -> 47.5 us
  local copies, waits for them, and re-layouts: 5.12 us -> 6.7 us
  Pallas kernels: 16.3 us -> 14.8 us
    ppermute x21 -> x22, waiting for transfers between devices: 50.4 us -> 37.5 us  [permute(): return lax.ppermute(x, axes, pairs) if pairs else jnp.zeros_like(x)]
    ppermute x21 -> x22, starting transfers between devices: 35.5 us -> 47.5 us  [permute(): return lax.ppermute(x, axes, pairs) if pairs else jnp.zeros_like(x)]
    pallas_call x10, Pallas kernels: 16.3 us -> 14.8 us  [call(): pl.pallas_call(kernel, out_shape=out_shapes, in_specs=[pl.BlockSpec(memor...]
  transfers between devices with their start and end apart: 21 -> 22, of which waited for: 11 -> 11; matrix products, arithmetic and copies ran while one was open for 1% -> 1% of each run, Pallas kernels for 13% -> 12%
where the time goes in v4:
time: 110 us; the launch traced here: 109 us
  starting transfers between devices  47.5 us (43%)
  waiting for transfers between devices  37.5 us (34%)
  Pallas kernels  14.8 us (13%)
  local copies, waits for them, and re-layouts  6.7 us (6%)
  between operations  1.6 us (1%)
    ppermute x22, starting transfers between devices, permute(): return lax.ppermute(x, axes, pairs) if pairs else jnp.zeros_like(x)  47.5 us
    ppermute x22, waiting for transfers between devices, permute(): return lax.ppermute(x, axes, pairs) if pairs else jnp.zeros_like(x)  37.5 us
    pallas_call x10, Pallas kernels, call(): pl.pallas_call(kernel, out_shape=out_shapes, in_specs=[pl.BlockSpec(memor...  14.8 us
    unnamed x24, local copies, waits for them, and re-layouts  4.82 us
  transfers between devices with their start and end apart: 22, of which 11 were waited for; matrix products, arithmetic and copies ran while one was open for 1% of the time, Pallas kernels for 12%

profile of v4, /device:TPU:13, one launch (start us, length us, event | category | flops | bytes accessed | tf_op | source)
XLA Modules:
  0.0 109.2 jit_solution(10336949144112885775)
XLA Ops:
  0.7 1.8 %dynamic-slice_bitcast_fusion = bf16[192,1024]{1,0:T(8,128)(2,1)} fusion(bf16[1,192,2048]{2,1,0:T(8,128)(2,1)} %param.7, s32[]{:T(128)S(6)} %select_n.89), kind=kLoop, calls=%fused_computation.5 | loop fusion | bytes 786436 | tf_op jit(solution)/shard_map/dynamic_slice | solution.py:331
  2.5 0.7 collective-permute-start
  3.8 0.1 fusion.3
  3.9 0.1 fusion.6
  4.0 0.1 stack.79
  4.1 0.1 select_reduce_fusion.flags
  4.2 0.0 copy-start.1
  4.2 1.2 %copy-done.1 = bf16[1,256,2048]{2,1,0:T(8,128)(2,1)S(1)} copy-done((bf16[1,256,2048]{2,1,0:T(8,128)(2,1)S(1)}, bf16[1,256,2048]{2,1,0:T(8,128)(2,1)}, u32[]{:S(2)}) %copy-start.1) | copy-done | bytes 1048600
  5.4 0.7 shard_map.78
  6.2 0.0 copy-start.3
  6.2 0.8 copy-done.3
  7.0 0.7 collective-permute-start.7
  7.7 0.7 collective-permute-start.5
  8.4 0.0 collective-permute-done.partner_part
  8.4 0.6 shard_map.76
  9.0 3.1 %collective-permute-start.1 = (bf16[192,1024]{1,0:T(8,128)(2,1)S(1)}, bf16[192,1024]{1,0:T(8,128)(2,1)S(1)}, u32[]{:S(2)}, u32[]{:S(2)}) collective-permute-start(bf16[192,1024]{1,0:T(8,128)(2,1)S(1)} %shard_map.76), channel_id=1, source_target_pairs={{0,8},{4,12},{8,16},{12,20},{16,24},{20,28},{1,9},{5,13},{9,17},{1... | collective-permute-start | bytes 1179656 | tf_op jit(solution)/shard_map/ppermute | solution.py:266
  12.1 1.6 %collective-permute-start.3 = (bf16[256,768]{1,0:T(8,128)(2,1)S(1)}, bf16[256,768]{1,0:T(8,128)(2,1)S(1)}, u32[]{:S(2)}, u32[]{:S(2)}) collective-permute-start(bf16[256,768]{1,0:T(8,128)(2,1)S(1)} %get-tuple-element.36.no.own_h), channel_id=1, source_target_pairs={{0,4},{4,0},{8,12},{12,8},{16,20},{20,16},{24,28},{28,24},{1,5},{5... | collective-permute-start | bytes 1179656 | tf_op jit(solution)/shard_map/ppermute | solution.py:266
  13.7 0.1 collective-permute-start.4
  13.8 0.0 collective-permute-done.7.yes
  13.8 0.6 shard_map.80
  14.4 7.6 %collective-permute-start.8 = (bf16[256,1024]{1,0:T(8,128)(2,1)S(1)}, bf16[256,1024]{1,0:T(8,128)(2,1)}, u32[]{:S(2)}, u32[]{:S(2)}) collective-permute-start(bf16[256,1024]{1,0:T(8,128)(2,1)S(1)} %shard_map.80), channel_id=1, source_target_pairs={{24,16},{4,12},{8,4},{20,24},{25,17},{5,13},{9,5},{21,25},{26,18},... | collective-permute-start | bytes 1572872 | tf_op jit(solution)/shard_map/ppermute | solution.py:266
  22.0 0.0 collective-permute-done.5.yes
  22.0 0.6 shard_map.79
  22.6 3.6 %collective-permute-start.6 = (bf16[256,768]{1,0:T(8,128)(2,1)S(1)}, bf16[256,768]{1,0:T(8,128)(2,1)}, u32[]{:S(2)}, u32[]{:S(2)}) collective-permute-start(bf16[256,768]{1,0:T(8,128)(2,1)S(1)} %shard_map.79), channel_id=1, source_target_pairs={{24,16},{4,12},{8,4},{20,24},{25,17},{5,13},{9,5},{21,25},{26,18},... | collective-permute-start | bytes 1179656 | tf_op jit(solution)/shard_map/ppermute | solution.py:266
  26.1 0.6 shard_map.77.u
  26.7 0.2 collective-permute-start.11
  27.0 0.7 copy-done.6
  27.7 2.4 %collective-permute-start.2 = (bf16[192,1024]{1,0:T(8,128)(2,1)S(1)}, bf16[192,1024]{1,0:T(8,128)(2,1)S(1)}, u32[]{:S(2)}, u32[]{:S(2)}) collective-permute-start(bf16[192,1024]{1,0:T(8,128)(2,1)S(1)} %shard_map.77.u), channel_id=1, source_target_pairs={{0,4},{1,2},{2,1},{3,7},{4,0},{5,6},{6,5},{7,3},{8,12},{9,10},{10,... | collective-permute-start | bytes 1179656 | tf_op jit(solution)/shard_map/ppermute | solution.py:266
  30.1 1.4 %collective-permute-done.6.from_h = bf16[256,768]{1,0:T(8,128)(2,1)} collective-permute-done((bf16[256,768]{1,0:T(8,128)(2,1)S(1)}, bf16[256,768]{1,0:T(8,128)(2,1)}, u32[]{:S(2)}, u32[]{:S(2)}) %collective-permute-start.6) | collective-permute-done | bytes 393248 | tf_op jit(solution)/shard_map/ppermute | solution.py:266
  31.5 0.0 collective-permute-done.8.from_c
  31.5 1.0 copy-done.4
  32.5 1.0 copy-done.7
  33.5 3.8 %shard_map.81 = (bf16[192,1024]{1,0:T(8,128)(2,1)S(1)}, bf16[192,1024]{1,0:T(8,128)(2,1)S(1)}, bf16[192,1024]{1,0:T(8,128)(2,1)S(1)}, bf16[192,1024]{1,0:T(8,128...) custom-call(s32[14]{0:T(128)S(1)} %select_reduce_fusion.flags, ...), custom_call_target="tpu_custom_call" | custom-call | flops 1207959552 | bytes 4325376 | tf_op jit(solution)/shard_map/pallas_call | solution.py:21
  37.3 0.1 collective-permute-done.11.a1
  37.4 1.3 %collective-permute-start.12 = (bf16[192,1024]{1,0:T(8,128)(2,1)S(1)}, bf16[192,1024]{1,0:T(8,128)(2,1)S(1)}, u32[]{:S(2)}, u32[]{:S(2)}) collective-permute-start(bf16[192,1024]{1,0:T(8,128)(2,1)S(1)} %collective-permute-done.11.a1), channel_id=1, source_target_pairs={{0,4},{1,2},{2,1},{3,7},{4,0},{5,6},{6,5},{7,3},{8,12},{9,10},{10,... | collective-permute-start | bytes 1179656 | tf_op jit(solution)/shard_map/ppermute | solution.py:266
  38.7 0.3 collective-permute-done.2.m1
  39.0 0.1 broadcast_select_fusion.1
  39.1 0.2 collective-permute-start.9
  39.2 7.4 %collective-permute-done.12.m2 = bf16[192,1024]{1,0:T(8,128)(2,1)S(1)} collective-permute-done((bf16[192,1024]{1,0:T(8,128)(2,1)S(1)}, bf16[192,1024]{1,0:T(8,128)(2,1)S(1)}, u32[]{:S(2)}, u32[]{:S(2)}) %collective-permute-start.12) | collective-permute-done | bytes 393248 | tf_op jit(solution)/shard_map/ppermute | solution.py:266
  46.6 0.1 collective-permute-start.13
  46.7 1.6 %collective-permute-done.9.a2 = bf16[192,1024]{1,0:T(8,128)(2,1)S(1)} collective-permute-done((bf16[192,1024]{1,0:T(8,128)(2,1)S(1)}, bf16[192,1024]{1,0:T(8,128)(2,1)S(1)}, u32[]{:S(2)}, u32[]{:S(2)}) %collective-permute-start.9) | collective-permute-done | bytes 393248 | tf_op jit(solution)/shard_map/ppermute | solution.py:266
  48.3 0.1 add_convert_fusion.3
  48.5 3.0 %collective-permute-start.10 = (bf16[192,1024]{1,0:T(8,128)(2,1)S(1)}, bf16[192,1024]{1,0:T(8,128)(2,1)S(1)}, u32[]{:S(2)}, u32[]{:S(2)}) collective-permute-start(bf16[192,1024]{1,0:T(8,128)(2,1)S(1)} %add_convert_fusion.3), channel_id=1, source_target_pairs={{0,4},{1,2},{2,1},{3,7},{4,0},{5,6},{6,5},{7,3},{8,12},{9,10},{10,... | collective-permute-start | bytes 1179656 | tf_op jit(solution)/shard_map/ppermute | solution.py:266
  51.5 5.3 %collective-permute-done.13.a3 = bf16[192,1024]{1,0:T(8,128)(2,1)S(1)} collective-permute-done((bf16[192,1024]{1,0:T(8,128)(2,1)S(1)}, bf16[192,1024]{1,0:T(8,128)(2,1)S(1)}, u32[]{:S(2)}, u32[]{:S(2)}) %collective-permute-start.13) | collective-permute-done | bytes 393248 | tf_op jit(solution)/shard_map/ppermute | solution.py:266
  56.8 0.1 add_convert_fusion.1
  56.9 2.0 %collective-permute-done.10 = bf16[192,1024]{1,0:T(8,128)(2,1)S(1)} collective-permute-done((bf16[192,1024]{1,0:T(8,128)(2,1)S(1)}, bf16[192,1024]{1,0:T(8,128)(2,1)S(1)}, u32[]{:S(2)}, u32[]{:S(2)}) %collective-permute-start.10) | collective-permute-done | bytes 393248 | tf_op jit(solution)/shard_map/ppermute | solution.py:266
  58.9 0.1 fusion
  59.0 0.1 collective-permute-start.14
  59.1 1.5 %collective-permute-start.15 = (bf16[192,1024]{1,0:T(8,128)(2,1)S(1)}, bf16[192,1024]{1,0:T(8,128)(2,1)S(1)}, u32[]{:S(2)}, u32[]{:S(2)}) collective-permute-start(bf16[192,1024]{1,0:T(8,128)(2,1)S(1)} %add_convert_fusion.1), channel_id=1, source_target_pairs={{0,4},{1,2},{2,1},{3,7},{4,0},{5,6},{6,5},{7,3},{8,12},{9,10},{10,... | collective-permute-start | bytes 1179656 | tf_op jit(solution)/shard_map/ppermute | solution.py:266
  60.6 3.8 %shard_map.82 = (bf16[256,1024]{1,0:T(8,128)(2,1)S(1)}, f32[256,768]{1,0:T(8,128)S(1)}, bf16[256,1792]{1,0:T(8,128)(2,1)S(1)}, bf16[256,1792]{1,0:T(8,128)(2,1)S(1)}) custom-call(s32[14]{0:T(128)S(1)} %select_reduce_fusion.flags, bf16[256,768]{1,0:T(8,128)(2,1)S(1)} %get-tuple-element.36.no.own_h, bf16[256,1024]{1,0:T(8,128)(2,1)S(1)} %copy-done.5, ...), custom_call_target="tpu_custom_call" | custom-call | flops 2415919104 | bytes 7077888 | tf_op jit(solution)/shard_map/pallas_call | solution.py:21
  64.5 2.6 %collective-permute-done.14 = bf16[192,1024]{1,0:T(8,128)(2,1)S(1)} collective-permute-done((bf16[192,1024]{1,0:T(8,128)(2,1)S(1)}, bf16[192,1024]{1,0:T(8,128)(2,1)S(1)}, u32[]{:S(2)}, u32[]{:S(2)}) %collective-permute-start.14) | collective-permute-done | bytes 393248 | tf_op jit(solution)/shard_map/ppermute | solution.py:266
  67.1 0.1 collective-permute-done.15
  67.2 0.2 add_convert_fusion.held
  67.4 3.2 %collective-permute-start.17 = (bf16[192,1024]{1,0:T(8,128)(2,1)S(1)}, bf16[192,1024]{1,0:T(8,128)(2,1)S(1)}, u32[]{:S(2)}, u32[]{:S(2)}) collective-permute-start(bf16[192,1024]{1,0:T(8,128)(2,1)S(1)} %add_convert_fusion.held), channel_id=1, source_target_pairs={{8,16},{12,28},{16,0},{20,12},{9,17},{13,29},{17,1},{21,13},{10,18... | collective-permute-start | bytes 1179656 | tf_op jit(solution)/shard_map/ppermute | solution.py:266
  70.6 7.4 %collective-permute-start.20 = (bf16[256,1792]{1,0:T(8,128)(2,1)S(1)}, bf16[256,1792]{1,0:T(8,128)(2,1)S(1)}, u32[]{:S(2)}, u32[]{:S(2)}) collective-permute-start(bf16[256,1792]{1,0:T(8,128)(2,1)S(1)} %get-tuple-element.55), channel_id=1, source_target_pairs={{0,4},{4,0},{8,12},{12,8},{16,20},{20,16},{24,28},{28,24},{1,5},{5... | collective-permute-start | bytes 2752520 | tf_op jit(solution)/shard_map/ppermute | solution.py:266
  78.0 1.3 %collective-permute-start.21 = (bf16[256,1792]{1,0:T(8,128)(2,1)S(1)}, bf16[256,1792]{1,0:T(8,128)(2,1)S(1)}, u32[]{:S(2)}, u32[]{:S(2)}) collective-permute-start(bf16[256,1792]{1,0:T(8,128)(2,1)S(1)} %get-tuple-element.56), channel_id=1, source_target_pairs={{4,8},{16,12},{12,16},{24,20},{5,9},{17,13},{13,17},{25,21},{6,10}... | collective-permute-start | bytes 2752520 | tf_op jit(solution)/shard_map/ppermute | solution.py:266
  79.3 0.1 collective-permute-start.16
  79.4 1.3 %collective-permute-start.18 = (bf16[192,1024]{1,0:T(8,128)(2,1)S(1)}, bf16[192,1024]{1,0:T(8,128)(2,1)S(1)}, u32[]{:S(2)}, u32[]{:S(2)}) collective-permute-start(bf16[192,1024]{1,0:T(8,128)(2,1)S(1)} %collective-permute-done.17.crossed), channel_id=1, source_target_pairs={{0,8},{28,20},{1,9},{29,21},{2,10},{30,22},{3,11},{31,23}} | collective-permute-start | bytes 1179656 | tf_op jit(solution)/shard_map/ppermute | solution.py:266
  80.7 8.7 %collective-permute-done.16.beside = bf16[192,1024]{1,0:T(8,128)(2,1)S(1)} collective-permute-done((bf16[192,1024]{1,0:T(8,128)(2,1)S(1)}, bf16[192,1024]{1,0:T(8,128)(2,1)S(1)}, u32[]{:S(2)}, u32[]{:S(2)}) %collective-permute-start.16) | collective-permute-done | bytes 393248 | tf_op jit(solution)/shard_map/ppermute | solution.py:266
  89.4 8.1 %collective-permute-done.18.relayed = bf16[192,1024]{1,0:T(8,128)(2,1)S(1)} collective-permute-done((bf16[192,1024]{1,0:T(8,128)(2,1)S(1)}, bf16[192,1024]{1,0:T(8,128)(2,1)S(1)}, u32[]{:S(2)}, u32[]{:S(2)}) %collective-permute-start.18) | collective-permute-done | bytes 393248 | tf_op jit(solution)/shard_map/ppermute | solution.py:266
  97.5 0.9 shard_map.83
  98.4 7.5 %collective-permute-start.19 = (bf16[192,1024]{1,0:T(8,128)(2,1)S(1)}, bf16[192,1024]{1,0:T(8,128)(2,1)S(1)}, u32[]{:S(2)}, u32[]{:S(2)}) collective-permute-start(bf16[192,1024]{1,0:T(8,128)(2,1)S(1)} %get-tuple-element.52), channel_id=1, source_target_pairs={{0,4},{4,0},{8,12},{12,8},{16,20},{20,16},{24,28},{28,24},{1,5},{5... | collective-permute-start | bytes 1179656 | tf_op jit(solution)/shard_map/ppermute | solution.py:266
  105.9 1.8 %shard_map.84 = (bf16[256,2048]{1,0:T(8,128)(2,1)}, bf16[256,768]{1,0:T(8,128)(2,1)}) custom-call(s32[14]{0:T(128)S(1)} %select_reduce_fusion.flags, bf16[256,1024]{1,0:T(8,128)(2,1)S(1)} %get-tuple-element.53.out, f32[256,768]{1,0:T(8,128)S(1)} %get-tuple-element.54.hg, bf16[256,1792]{1,0:T(8,128)(2,1)S(1)} %collective-permute-done.20.core, ...), custom_call_target="tpu_custom_call" | custom-call | bytes 3670016 | tf_op jit(solution)/shard_map/pallas_call | solution.py:21
  107.7 1.5 %shard_map.85 = bf16[192,2048]{1,0:T(8,128)(2,1)} custom-call(s32[14]{0:T(128)S(1)} %select_reduce_fusion.flags, bf16[192,1024]{1,0:T(8,128)(2,1)S(1)} %get-tuple-element.61.own, bf16[192,1024]{1,0:T(8,128)(2,1)S(1)} %collective-permute-done.19.other), custom_call_target="tpu_custom_call" | custom-call | bytes 1572864 | tf_op jit(solution)/shard_map/pallas_call | solution.py:21
  (31 shorter events, 0.1 us)
Async XLA Ops:
  0.6 3.2 %copy-start.11 = (s32[8]{0:T(128)S(1)}, s32[8]{0:T(128)}, u32[]{:S(2)}) copy-start(s32[8]{0:T(128)} %param.8) | copy-start | bytes 100
  0.7 3.6 %copy-start.2 = (bf16[1,256,768]{2,1,0:T(8,128)(2,1)S(1)}, bf16[1,256,768]{2,1,0:T(8,128)(2,1)}, u32[]{:S(2)}) copy-start(bf16[1,256,768]{2,1,0:T(8,128)(2,1)} %param.5) | copy-start | bytes 1179652
  2.5 5.9 %copy-start = (bf16[1,192,2048]{2,1,0:T(8,128)(2,1)S(1)}, bf16[1,192,2048]{2,1,0:T(8,128)(2,1)}, u32[]{:S(2)}) copy-start(bf16[1,192,2048]{2,1,0:T(8,128)(2,1)} %param.7) | copy-start | bytes 2359300
  2.5 5.9 %collective-permute-start = (bf16[192,1024]{1,0:T(8,128)(2,1)}, bf16[192,1024]{1,0:T(8,128)(2,1)S(1)}, u32[]{:S(2)}, u32[]{:S(2)}) collective-permute-start(bf16[192,1024]{1,0:T(8,128)(2,1)} %dynamic-slice_bitcast_fusion), channel_id=1, source_target_pairs={{0,4},{4,0},{8,12},{12,8},{16,20},{20,16},{24,28},{28,24},{1,5},{5... | collective-permute-start | bytes 1179656 | tf_op jit(solution)/shard_map/ppermute | solution.py:266
  4.2 1.2 %copy-start.1 = (bf16[1,256,2048]{2,1,0:T(8,128)(2,1)S(1)}, bf16[1,256,2048]{2,1,0:T(8,128)(2,1)}, u32[]{:S(2)}) copy-start(bf16[1,256,2048]{2,1,0:T(8,128)(2,1)} %param.6) | copy-start | bytes 3145732
  6.2 0.8 copy-start.3
  7.0 6.8 %collective-permute-start.7 = (bf16[256,1024]{1,0:T(8,128)(2,1)S(1)}, bf16[256,1024]{1,0:T(8,128)(2,1)S(1)}, u32[]{:S(2)}, u32[]{:S(2)}) collective-permute-start(bf16[256,1024]{1,0:T(8,128)(2,1)S(1)} %get-tuple-element.38.no), channel_id=1, source_target_pairs={{12,24},{16,4},{13,25},{17,5},{14,26},{18,6},{15,27},{19,7}} | collective-permute-start | bytes 1572872 | tf_op jit(solution)/shard_map/ppermute | solution.py:266
  7.7 14.3 %collective-permute-start.5 = (bf16[256,768]{1,0:T(8,128)(2,1)S(1)}, bf16[256,768]{1,0:T(8,128)(2,1)S(1)}, u32[]{:S(2)}, u32[]{:S(2)}) collective-permute-start(bf16[256,768]{1,0:T(8,128)(2,1)S(1)} %get-tuple-element.36.no.own_h), channel_id=1, source_target_pairs={{12,24},{16,4},{13,25},{17,5},{14,26},{18,6},{15,27},{19,7}} | collective-permute-start | bytes 1179656 | tf_op jit(solution)/shard_map/ppermute | solution.py:266
  9.0 17.1 %collective-permute-start.1 = (bf16[192,1024]{1,0:T(8,128)(2,1)S(1)}, bf16[192,1024]{1,0:T(8,128)(2,1)S(1)}, u32[]{:S(2)}, u32[]{:S(2)}) collective-permute-start(bf16[192,1024]{1,0:T(8,128)(2,1)S(1)} %shard_map.76), channel_id=1, source_target_pairs={{0,8},{4,12},{8,16},{12,20},{16,24},{20,28},{1,9},{5,13},{9,17},{1... | collective-permute-start | bytes 1179656 | tf_op jit(solution)/shard_map/ppermute | solution.py:266
  12.1 14.8 %collective-permute-start.3 = (bf16[256,768]{1,0:T(8,128)(2,1)S(1)}, bf16[256,768]{1,0:T(8,128)(2,1)S(1)}, u32[]{:S(2)}, u32[]{:S(2)}) collective-permute-start(bf16[256,768]{1,0:T(8,128)(2,1)S(1)} %get-tuple-element.36.no.own_h), channel_id=1, source_target_pairs={{0,4},{4,0},{8,12},{12,8},{16,20},{20,16},{24,28},{28,24},{1,5},{5... | collective-permute-start | bytes 1179656 | tf_op jit(solution)/shard_map/ppermute | solution.py:266
  13.7 16.4 %collective-permute-start.4 = (bf16[256,1024]{1,0:T(8,128)(2,1)S(1)}, bf16[256,1024]{1,0:T(8,128)(2,1)}, u32[]{:S(2)}, u32[]{:S(2)}) collective-permute-start(bf16[256,1024]{1,0:T(8,128)(2,1)S(1)} %get-tuple-element.38.no), channel_id=1, source_target_pairs={{0,4},{4,0},{8,12},{12,8},{16,20},{20,16},{24,28},{28,24},{1,5},{5... | collective-permute-start | bytes 1572872 | tf_op jit(solution)/shard_map/ppermute | solution.py:266
  14.4 17.1 %collective-permute-start.8 = (bf16[256,1024]{1,0:T(8,128)(2,1)S(1)}, bf16[256,1024]{1,0:T(8,128)(2,1)}, u32[]{:S(2)}, u32[]{:S(2)}) collective-permute-start(bf16[256,1024]{1,0:T(8,128)(2,1)S(1)} %shard_map.80), channel_id=1, source_target_pairs={{24,16},{4,12},{8,4},{20,24},{25,17},{5,13},{9,5},{21,25},{26,18},... | collective-permute-start | bytes 1572872 | tf_op jit(solution)/shard_map/ppermute | solution.py:266
  22.6 8.9 %collective-permute-start.6 = (bf16[256,768]{1,0:T(8,128)(2,1)S(1)}, bf16[256,768]{1,0:T(8,128)(2,1)}, u32[]{:S(2)}, u32[]{:S(2)}) collective-permute-start(bf16[256,768]{1,0:T(8,128)(2,1)S(1)} %shard_map.79), channel_id=1, source_target_pairs={{24,16},{4,12},{8,4},{20,24},{25,17},{5,13},{9,5},{21,25},{26,18},... | collective-permute-start | bytes 1179656 | tf_op jit(solution)/shard_map/ppermute | solution.py:266
  26.7 10.7 %collective-permute-start.11 = (bf16[192,1024]{1,0:T(8,128)(2,1)S(1)}, bf16[192,1024]{1,0:T(8,128)(2,1)S(1)}, u32[]{:S(2)}, u32[]{:S(2)}) collective-permute-start(bf16[192,1024]{1,0:T(8,128)(2,1)S(1)} %shard_map.77.u), channel_id=1, source_target_pairs={{0,1},{1,0},{2,3},{3,2},{4,5},{5,4},{6,7},{7,6},{8,9},{9,8},{10,11... | collective-permute-start | bytes 1179656 | tf_op jit(solution)/shard_map/ppermute | solution.py:266
  27.0 0.7 copy-start.6
  27.7 11.3 %collective-permute-start.2 = (bf16[192,1024]{1,0:T(8,128)(2,1)S(1)}, bf16[192,1024]{1,0:T(8,128)(2,1)S(1)}, u32[]{:S(2)}, u32[]{:S(2)}) collective-permute-start(bf16[192,1024]{1,0:T(8,128)(2,1)S(1)} %shard_map.77.u), channel_id=1, source_target_pairs={{0,4},{1,2},{2,1},{3,7},{4,0},{5,6},{6,5},{7,3},{8,12},{9,10},{10,... | collective-permute-start | bytes 1179656 | tf_op jit(solution)/shard_map/ppermute | solution.py:266
  31.5 1.0 copy-start.4
  32.5 1.0 copy-start.7
  37.4 1.6 %copy-start.9 = (bf16[192,1024]{1,0:T(8,128)(2,1)}, bf16[192,1024]{1,0:T(8,128)(2,1)S(1)}, u32[]{:S(2)}) copy-start(bf16[192,1024]{1,0:T(8,128)(2,1)S(1)} %collective-permute-done.11.a1) | copy-start | bytes 1179652
  37.4 9.2 %collective-permute-start.12 = (bf16[192,1024]{1,0:T(8,128)(2,1)S(1)}, bf16[192,1024]{1,0:T(8,128)(2,1)S(1)}, u32[]{:S(2)}, u32[]{:S(2)}) collective-permute-start(bf16[192,1024]{1,0:T(8,128)(2,1)S(1)} %collective-permute-done.11.a1), channel_id=1, source_target_pairs={{0,4},{1,2},{2,1},{3,7},{4,0},{5,6},{6,5},{7,3},{8,12},{9,10},{10,... | collective-permute-start | bytes 1179656 | tf_op jit(solution)/shard_map/ppermute | solution.py:266
  39.1 9.2 %collective-permute-start.9 = (bf16[192,1024]{1,0:T(8,128)(2,1)S(1)}, bf16[192,1024]{1,0:T(8,128)(2,1)S(1)}, u32[]{:S(2)}, u32[]{:S(2)}) collective-permute-start(bf16[192,1024]{1,0:T(8,128)(2,1)S(1)} %broadcast_select_fusion.1), channel_id=1, source_target_pairs={{0,1},{1,0},{2,3},{3,2},{4,5},{5,4},{6,7},{7,6},{8,9},{9,8},{10,11... | collective-permute-start | bytes 1179656 | tf_op jit(solution)/shard_map/ppermute | solution.py:266
  46.6 10.1 %collective-permute-start.13 = (bf16[192,1024]{1,0:T(8,128)(2,1)S(1)}, bf16[192,1024]{1,0:T(8,128)(2,1)S(1)}, u32[]{:S(2)}, u32[]{:S(2)}) collective-permute-start(bf16[192,1024]{1,0:T(8,128)(2,1)S(1)} %broadcast_select_fusion), channel_id=1, source_target_pairs={{0,1},{1,0},{2,3},{3,2},{4,5},{5,4},{6,7},{7,6},{8,9},{9,8},{10,11... | collective-permute-start | bytes 1179656 | tf_op jit(solution)/shard_map/ppermute | solution.py:266
  48.5 10.4 %collective-permute-start.10 = (bf16[192,1024]{1,0:T(8,128)(2,1)S(1)}, bf16[192,1024]{1,0:T(8,128)(2,1)S(1)}, u32[]{:S(2)}, u32[]{:S(2)}) collective-permute-start(bf16[192,1024]{1,0:T(8,128)(2,1)S(1)} %add_convert_fusion.3), channel_id=1, source_target_pairs={{0,4},{1,2},{2,1},{3,7},{4,0},{5,6},{6,5},{7,3},{8,12},{9,10},{10,... | collective-permute-start | bytes 1179656 | tf_op jit(solution)/shard_map/ppermute | solution.py:266
  56.8 3.9 %copy-start.10 = (bf16[192,1024]{1,0:T(8,128)(2,1)S(1)}, bf16[192,1024]{1,0:T(8,128)(2,1)}, u32[]{:S(2)}) copy-start(bf16[192,1024]{1,0:T(8,128)(2,1)} %copy-done.9) | copy-start | bytes 1179652
  58.9 1.8 %copy-start.5 = (bf16[256,1024]{1,0:T(8,128)(2,1)S(1)}, bf16[256,1024]{1,0:T(8,128)(2,1)}, u32[]{:S(2)}) copy-start(bf16[256,1024]{1,0:T(8,128)(2,1)} %copy-done.3) | copy-start | bytes 1572868
  58.9 1.8 %copy-start.8 = (bf16[256,768]{1,0:T(8,128)(2,1)S(1)}, bf16[256,768]{1,0:T(8,128)(2,1)}, u32[]{:S(2)}) copy-start(bf16[256,768]{1,0:T(8,128)(2,1)} %copy-done.6) | copy-start | bytes 1179652
  59.0 8.1 %collective-permute-start.14 = (bf16[192,1024]{1,0:T(8,128)(2,1)S(1)}, bf16[192,1024]{1,0:T(8,128)(2,1)S(1)}, u32[]{:S(2)}, u32[]{:S(2)}) collective-permute-start(bf16[192,1024]{1,0:T(8,128)(2,1)S(1)} %fusion), channel_id=1, source_target_pairs={{0,1},{1,0},{2,3},{3,2},{4,5},{5,4},{6,7},{7,6},{8,9},{9,8},{10,11... | collective-permute-start | bytes 1179656 | tf_op jit(solution)/shard_map/ppermute | solution.py:266
  59.1 8.1 %collective-permute-start.15 = (bf16[192,1024]{1,0:T(8,128)(2,1)S(1)}, bf16[192,1024]{1,0:T(8,128)(2,1)S(1)}, u32[]{:S(2)}, u32[]{:S(2)}) collective-permute-start(bf16[192,1024]{1,0:T(8,128)(2,1)S(1)} %add_convert_fusion.1), channel_id=1, source_target_pairs={{0,4},{1,2},{2,1},{3,7},{4,0},{5,6},{6,5},{7,3},{8,12},{9,10},{10,... | collective-permute-start | bytes 1179656 | tf_op jit(solution)/shard_map/ppermute | solution.py:266
  67.4 12.0 %collective-permute-start.17 = (bf16[192,1024]{1,0:T(8,128)(2,1)S(1)}, bf16[192,1024]{1,0:T(8,128)(2,1)S(1)}, u32[]{:S(2)}, u32[]{:S(2)}) collective-permute-start(bf16[192,1024]{1,0:T(8,128)(2,1)S(1)} %add_convert_fusion.held), channel_id=1, source_target_pairs={{8,16},{12,28},{16,0},{20,12},{9,17},{13,29},{17,1},{21,13},{10,18... | collective-permute-start | bytes 1179656 | tf_op jit(solution)/shard_map/ppermute | solution.py:266
  70.6 35.3 %collective-permute-start.20 = (bf16[256,1792]{1,0:T(8,128)(2,1)S(1)}, bf16[256,1792]{1,0:T(8,128)(2,1)S(1)}, u32[]{:S(2)}, u32[]{:S(2)}) collective-permute-start(bf16[256,1792]{1,0:T(8,128)(2,1)S(1)} %get-tuple-element.55), channel_id=1, source_target_pairs={{0,4},{4,0},{8,12},{12,8},{16,20},{20,16},{24,28},{28,24},{1,5},{5... | collective-permute-start | bytes 2752520 | tf_op jit(solution)/shard_map/ppermute | solution.py:266
  78.0 27.9 %collective-permute-start.21 = (bf16[256,1792]{1,0:T(8,128)(2,1)S(1)}, bf16[256,1792]{1,0:T(8,128)(2,1)S(1)}, u32[]{:S(2)}, u32[]{:S(2)}) collective-permute-start(bf16[256,1792]{1,0:T(8,128)(2,1)S(1)} %get-tuple-element.56), channel_id=1, source_target_pairs={{4,8},{16,12},{12,16},{24,20},{5,9},{17,13},{13,17},{25,21},{6,10}... | collective-permute-start | bytes 2752520 | tf_op jit(solution)/shard_map/ppermute | solution.py:266
  79.3 10.1 %collective-permute-start.16 = (bf16[192,1024]{1,0:T(8,128)(2,1)S(1)}, bf16[192,1024]{1,0:T(8,128)(2,1)S(1)}, u32[]{:S(2)}, u32[]{:S(2)}) collective-permute-start(bf16[192,1024]{1,0:T(8,128)(2,1)S(1)} %add_convert_fusion.held), channel_id=1, source_target_pairs={{0,8},{4,12},{8,0},{12,4},{16,24},{20,28},{24,16},{28,20},{1,9},{5... | collective-permute-start | bytes 1179656 | tf_op jit(solution)/shard_map/ppermute | solution.py:266
  79.4 18.1 %collective-permute-start.18 = (bf16[192,1024]{1,0:T(8,128)(2,1)S(1)}, bf16[192,1024]{1,0:T(8,128)(2,1)S(1)}, u32[]{:S(2)}, u32[]{:S(2)}) collective-permute-start(bf16[192,1024]{1,0:T(8,128)(2,1)S(1)} %collective-permute-done.17.crossed), channel_id=1, source_target_pairs={{0,8},{28,20},{1,9},{29,21},{2,10},{30,22},{3,11},{31,23}} | collective-permute-start | bytes 1179656 | tf_op jit(solution)/shard_map/ppermute | solution.py:266
  98.4 9.3 %collective-permute-start.19 = (bf16[192,1024]{1,0:T(8,128)(2,1)S(1)}, bf16[192,1024]{1,0:T(8,128)(2,1)S(1)}, u32[]{:S(2)}, u32[]{:S(2)}) collective-permute-start(bf16[192,1024]{1,0:T(8,128)(2,1)S(1)} %get-tuple-element.52), channel_id=1, source_target_pairs={{0,4},{4,0},{8,12},{12,8},{16,20},{20,16},{24,28},{28,24},{1,5},{5... | collective-permute-start | bytes 1179656 | tf_op jit(solution)/shard_map/ppermute | solution.py:266
